TPU v7x, 256 devices: a whole 4x4x8 slice. The times are simulated.
256 devices in a mesh: leaf: 32 (over x, z), row: 8 (over y, core).
Axes of the slice: x: 4, y: 4, z: 8, core: 2. Of those that a mesh axis runs over, the one named last changes fastest.
Arguments:
- leaf_probes: bfloat16 [32, 2048, 128], P('leaf', 'row'), may hold values from -6 to 6
- lower_probes: bfloat16 [4, 4096, 128], P(None, ('leaf', 'row')), may hold values from -6 to 6
- middle_probes: bfloat16 [2, 8192, 128], P(None, ('leaf', 'row')), may hold values from -6 to 6
- root_probes: bfloat16 [16384, 128], P(('leaf', 'row')), may hold values from -6 to 6
- leaf_inverse: bfloat16 [32, 2048, 2048], P('leaf', 'row'), as said below
- lower_inverse: bfloat16 [4, 4096, 4096], P(None, 'row', 'leaf'), as said below
- middle_inverse: bfloat16 [2, 8192, 8192], P(None, 'row', 'leaf'), as said below
- root_inverse: bfloat16 [16384, 16384], P('row', 'leaf'), as said below
- leaf_panel: bfloat16 [32, 512, 2048], P('leaf', 'row'), may hold values from -0.09375 to 0.09375
- lower_to_middle: bfloat16 [4, 8192, 4096], P(None, 'leaf', 'row'), may hold values from -0.125 to 0.125
- lower_to_root: bfloat16 [4, 16384, 4096], P(None, 'leaf', 'row'), may hold values from -0.125 to 0.125
- middle_to_root: bfloat16 [2, 16384, 8192], P(None, 'leaf', 'row'), may hold values from -0.09375 to 0.09375
- leaf_parent: int32 [32], replicated, may hold values from 0 to 3
- leaf_blocks: int32 [32, 4], replicated, may hold values from 0 to 127, as said below
Outputs:
- leaf_solution: bfloat16 [32, 2048, 128], P('leaf', 'row')
- lower_solution: bfloat16 [4, 4096, 128], P(None, ('leaf', 'row'))
- middle_solution: bfloat16 [2, 8192, 128], P(None, ('leaf', 'row'))
- root_solution: bfloat16 [16384, 128], P(('leaf', 'row'))
Inputs may be any that keep to these rules, and one draw needn't show every extreme that they name: `leaf_inverse`: every inverse of a diagonal factor block is lower triangular: entries above its diagonal are zero. `lower_inverse`: every inverse of a diagonal factor block is lower triangular: entries above its diagonal are zero. `middle_inverse`: every inverse of a diagonal factor block is lower triangular: entries above its diagonal are zero. `root_inverse`: every inverse of a diagonal factor block is lower triangular: entries above its diagonal are zero. `leaf_blocks`: columns 0 and 1 are two different blocks of 128 rows of the parent separator, column 2 a block of the second-level separator above it, column 3 a block of the root.
All inputs are finite; a program needn't handle non-finite values.
Results may differ from a plain program's by a relative error of at most 0.04.
Values may be sent and summed in bfloat16 or wider, within the bound.
No kernel may reach another device: no remote copies, remote signals or barrier semaphores. Data moves between devices by JAX's collectives and lax.ppermute only.
A program may use at most 64 MiB of HBM per device.

v0:
```python
import jax
import jax.numpy as jnp
from jax import lax
from jax.experimental import pallas as pl
from jax.experimental.pallas import tpu as pltpu
from jax.sharding import Mesh, PartitionSpec as P

LEAF = ("x", "z")
ROW = ("y", "core")
LEAVES = 32
ROWS = 8
HALF = 64
F32 = jnp.float32
BF16 = jnp.bfloat16


def swap(pieces, axes):
    return lax.all_to_all(pieces, axes, split_axis=0, concat_axis=0, tiled=True)


def total(pieces):
    return jnp.sum(pieces.astype(F32), axis=0)


def copies(piece, count):
    return jnp.broadcast_to(piece[None], (count,) + piece.shape)


def leaf_terms(partial):
    return swap(partial.reshape(LEAVES, HALF, -1), LEAF)


def leaf_gather(piece):
    return swap(copies(piece.astype(BF16), LEAVES), LEAF)


def z_terms(partial):
    return swap(partial.reshape(8, HALF, -1), "z")


def z_gather(piece):
    return swap(copies(piece, 8), "z").reshape((-1,) + piece.shape[1:])


def shift(piece, axis, step):
    return lax.ppermute(piece, axis, [(i, (i + step) % 4) for i in range(4)])


def both_cores(piece):
    return lax.all_gather(piece, "core", axis=0, tiled=False)


def row_gather(piece):
    return both_cores(swap(copies(piece, 4), "y"))


def row_half_sum(partial, core):
    halves = lax.dynamic_slice_in_dim(both_cores(partial), core * 256, 256, axis=1)
    pair = total(halves).astype(BF16)
    others = [shift(pair, "y", step) for step in (1, 2, 3)]
    return sum([piece.astype(F32) for piece in others], pair.astype(F32))


def row_scatter(partial, core):
    halves = partial.reshape(4, 2, 256, -1)
    mine = jnp.where(core == 0, halves[:, 0], halves[:, 1])
    theirs = jnp.where(core == 0, halves[:, 1], halves[:, 0])
    pair = mine.astype(F32) + lax.ppermute(theirs, "core", [(0, 1), (1, 0)]).astype(F32)
    return total(swap(pair.astype(BF16), "y"))


def product(left, right):
    return jnp.dot(left, right, preferred_element_type=F32)


LIMITS = pltpu.CompilerParams(vmem_limit_bytes=12 * 1024 * 1024)


def forward(matrix, columns, rows_at_once=512):
    count, rows, depth = matrix.shape
    probes = columns.shape[-1]
    step = min(rows, rows_at_once)

    def kernel(matrix_ref, columns_ref, out_ref):
        out_ref[0] = product(matrix_ref[0], columns_ref[0]).astype(BF16)

    return pl.pallas_call(
        kernel,
        out_shape=jax.ShapeDtypeStruct((count, rows, probes), BF16),
        grid=(count, rows // step),
        in_specs=[
            pl.BlockSpec((1, step, depth), lambda s, m: (s, m, 0)),
            pl.BlockSpec((1, depth, probes), lambda s, m: (s, 0, 0)),
        ],
        out_specs=pl.BlockSpec((1, step, probes), lambda s, m: (s, m, 0)),
        compiler_params=LIMITS,
        name="forward",
    )(matrix, columns)


def forward_total(matrix, columns, start, group, dtype):
    count, rows, depth = matrix.shape
    probes = columns.shape[-1]

    def kernel(matrix_ref, columns_ref, start_ref, out_ref, sum_ref):
        member = pl.program_id(0) % group

        @pl.when(member == 0)
        def _():
            sum_ref[...] = start_ref[0]

        sum_ref[...] += product(matrix_ref[0], columns_ref[0])

        @pl.when(member == group - 1)
        def _():
            out_ref[0] = sum_ref[...].astype(dtype)

    in_specs = [
        pl.BlockSpec((1, rows, depth), lambda s: (s, 0, 0)),
        pl.BlockSpec((1, depth, probes), lambda s: (s, 0, 0)),
        pl.BlockSpec((1, rows, probes), lambda s: (s // group, 0, 0)),
    ]
    return pl.pallas_call(
        kernel,
        out_shape=jax.ShapeDtypeStruct((count // group, rows, probes), dtype),
        grid=(count,),
        in_specs=in_specs,
        out_specs=pl.BlockSpec((1, rows, probes), lambda s: (s // group, 0, 0)),
        scratch_shapes=[pltpu.VMEM((rows, probes), F32)],
        compiler_params=LIMITS,
        name="forward_total",
    )(matrix, columns, start)


def backward(matrix, rows_in, depth_at_once=512):
    count, depth, width = matrix.shape
    probes = rows_in.shape[-1]
    step = min(depth, depth_at_once)
    steps = depth // step

    def kernel(matrix_ref, rows_ref, out_ref, sum_ref):
        at = pl.program_id(1)

        @pl.when(at == 0)
        def _():
            sum_ref[...] = jnp.zeros_like(sum_ref)

        sum_ref[...] += product(rows_ref[0].T, matrix_ref[0])

        @pl.when(at == steps - 1)
        def _():
            out_ref[0] = sum_ref[...].T.astype(BF16)

    return pl.pallas_call(
        kernel,
        out_shape=jax.ShapeDtypeStruct((count, width, probes), BF16),
        grid=(count, steps),
        in_specs=[
            pl.BlockSpec((1, step, width), lambda s, m: (s, m, 0)),
            pl.BlockSpec((1, step, probes), lambda s, m: (s, m, 0)),
        ],
        out_specs=pl.BlockSpec((1, width, probes), lambda s, m: (s, 0, 0)),
        scratch_shapes=[pltpu.VMEM((probes, width), F32)],
        compiler_params=LIMITS,
        name="backward",
    )(matrix, rows_in)


def backward_lower(to_middle, middle_rows, to_root, root_rows):
    count, middle_depth, width = to_middle.shape
    root_depth = to_root.shape[1]
    probes = root_rows.shape[-1]

    def kernel(middle_ref, middle_rows_ref, root_ref, root_rows_ref, out_ref):
        both = product(root_rows_ref[...].T, root_ref[0]) + product(middle_rows_ref[0].T, middle_ref[0])
        out_ref[0] = both.T.astype(BF16)

    return pl.pallas_call(
        kernel,
        out_shape=jax.ShapeDtypeStruct((count, width, probes), BF16),
        grid=(count,),
        in_specs=[
            pl.BlockSpec((1, middle_depth, width), lambda s: (s, 0, 0)),
            pl.BlockSpec((1, middle_depth, probes), lambda s: (s // 2, 0, 0)),
            pl.BlockSpec((1, root_depth, width), lambda s: (s, 0, 0)),
            pl.BlockSpec((root_depth, probes), lambda s: (0, 0)),
        ],
        out_specs=pl.BlockSpec((1, width, probes), lambda s: (s, 0, 0)),
        compiler_params=LIMITS,
        name="backward_lower",
    )(to_middle, middle_rows, to_root, root_rows)


def pieces_product(matrix, held, times):
    rows, probes = matrix.shape[0], held.shape[-1]

    def kernel(matrix_ref, held_ref, out_ref):
        result = jnp.zeros((rows, probes), F32)
        for y in range(4):
            for core in range(2):
                at = (2 * y + core) * 256
                result += product(matrix_ref[:, at : at + 256], held_ref[core, y])
        rounded = result.astype(BF16)
        for copy in range(times):
            out_ref[copy] = rounded

    return pl.pallas_call(
        kernel,
        out_shape=jax.ShapeDtypeStruct((times, rows, probes), BF16),
        grid=(1,),
        in_specs=[
            pl.BlockSpec((rows, matrix.shape[1]), lambda i: (0, 0)),
            pl.BlockSpec((2, 4, 256, probes), lambda i: (0, 0, 0, 0)),
        ],
        out_specs=pl.BlockSpec((times, rows, probes), lambda i: (0, 0, 0)),
        compiler_params=LIMITS,
        name="pieces_product",
    )(matrix, held)


def body(
    leaf_probes,
    lower_probes,
    middle_probes,
    root_probes,
    leaf_inverse,
    lower_inverse,
    middle_inverse,
    root_inverse,
    leaf_panel,
    lower_to_middle,
    lower_to_root,
    middle_to_root,
    leaf_parent,
    leaf_blocks,
):
    x = lax.axis_index("x")
    z = lax.axis_index("z")
    leaf = x * 8 + z
    y = lax.axis_index("y")
    core = lax.axis_index("core")
    row = y * 2 + core
    probes = leaf_probes.shape[-1]
    inverse = leaf_inverse[0]
    panel = leaf_panel[0]

    lower_held = jnp.concatenate([lower_inverse, lower_probes], axis=1)
    leaving = [lax.dynamic_index_in_dim(lower_held, (x + step) % 4, axis=0, keepdims=False) for step in range(4)]
    leaf_probes, leaving = lax.optimization_barrier((leaf_probes, leaving))
    lower_tiles = [leaving[0]] + [shift(leaving[step], "x", step) for step in (1, 2, 3)]

    block = lax.dynamic_index_in_dim(leaf_blocks, y, axis=1, keepdims=False)
    parent = leaf_parent
    slot = jnp.where(
        y < 2,
        jnp.where((parent == x) & (block % 8 == z), (x + 4 - block // 8) % 4, -1),
        jnp.where(
            y == 2,
            jnp.where(block // 2 == leaf, (parent // 2) * 2 + block % 2, -1),
            jnp.where(block // 4 == leaf, block % 4, -1),
        ),
    )
    chosen = (slot[None, :] == jnp.arange(4, dtype=jnp.int32)[:, None]).astype(F32)

    held = row_gather(leaf_probes[0])
    leaf_solved = pieces_product(inverse, held, 1)[0]
    updates = pieces_product(panel, row_gather(leaf_solved), LEAVES)
    received, lower_tiles = lax.optimization_barrier((swap(updates, LEAF), lower_tiles))
    lower_square = jnp.concatenate([tile[:512] for tile in lower_tiles], axis=1)[None]
    lower_pieces = jnp.concatenate([tile[512:] for tile in lower_tiles])
    received = received.astype(F32)
    landed = jnp.sum(chosen[:, :, None, None] * received[None], axis=1).astype(BF16)
    by_level = swap(copies(jnp.concatenate([landed.reshape(-1, probes), lower_pieces]), 4), "y")
    added = by_level[:, :256].reshape(4, 4, HALF, probes)
    lower_added = (added[0].astype(F32) + added[1].astype(F32)).astype(BF16)
    by_half = both_cores(jnp.concatenate([lower_added, by_level[:, 256:]]))
    lower_added = by_half[:, :4].transpose(1, 0, 2, 3).reshape(4, 128, probes)
    lower_own = by_half[:, 4:].reshape(2, 4, 4, 16, probes).transpose(2, 1, 0, 3, 4).reshape(4, 128, probes)
    lower_input = (lower_own.astype(F32) - lower_added.astype(F32)).astype(BF16).reshape(1, 512, probes)

    half_ids = lax.broadcasted_iota(jnp.int32, (1, 2, 1, 1), 1)
    row_ids = lax.broadcasted_iota(jnp.int32, (1, ROWS, 1, 1), 1)

    def contribution(level, own_probes):
        placed = jnp.where((half_ids == core) & (y == level), landed[:, None].astype(F32), 0.0)
        own = jnp.where(row_ids == row, own_probes[:, None].astype(F32), 0.0)
        return placed.reshape(own_probes.shape[0], -1, probes) - own.reshape(own_probes.shape[0], -1, probes)

    middle_start = contribution(2, middle_probes)
    root_start = contribution(3, root_probes[None])

    lower_terms = z_terms(forward(lower_square, lower_input))
    lower_gathered = leaf_gather(total(lower_terms))
    lower_solved = lax.dynamic_index_in_dim(lower_gathered, leaf, axis=0, keepdims=False)
    lower_block = lower_gathered.reshape(4, 512, probes)
    to_middle = forward_total(lower_to_middle, lower_block, middle_start, 2, BF16).reshape(512, probes)
    middle_input = both_cores((-row_half_sum(to_middle, core)).astype(BF16))
    to_root = forward_total(lower_to_root, lower_block, root_start, 4, F32)

    middle_terms = leaf_terms(forward(middle_inverse, middle_input))
    middle_gathered = leaf_gather(total(middle_terms))
    middle_solved = lax.dynamic_index_in_dim(middle_gathered, leaf, axis=0, keepdims=False)
    middle_block = middle_gathered.reshape(2, 1024, probes)
    to_root = forward_total(middle_to_root, middle_block, to_root, 2, BF16).reshape(512, probes)
    root_input = both_cores((-row_half_sum(to_root, core)).astype(BF16)).reshape(1, 512, probes)

    root_terms = leaf_terms(forward(root_inverse[None], root_input))
    root_rows = leaf_gather(total(root_terms)).reshape(1, 2048, probes)
    root_half = row_half_sum(backward(root_inverse[None], root_rows)[0], core).astype(BF16)
    root_columns = both_cores(root_half).reshape(512, probes)

    middle_drop = leaf_terms(backward(middle_to_root, jnp.broadcast_to(root_columns[None], (2, 512, probes))))
    middle_rows = leaf_gather(middle_solved.astype(F32) - total(middle_drop)).reshape(2, 1024, probes)
    middle_half = row_half_sum(backward(middle_inverse, middle_rows).reshape(512, probes), core).astype(BF16)
    middle_columns = both_cores(middle_half)

    lower_drop = backward_lower(lower_to_middle, middle_columns, lower_to_root, root_columns)
    lower_rows = z_gather((lower_solved.astype(F32) - total(leaf_terms(lower_drop))).astype(BF16))
    lower_half = row_half_sum(backward(lower_square, lower_rows[None])[0], core)
    lower_columns = both_cores(lower_half.astype(BF16)).reshape(4, 128, probes)

    stacked = jnp.where(
        y < 2,
        lower_columns.reshape(4, 2, HALF, probes),
        jnp.where(
            y == 2,
            middle_columns.reshape(4, 2, HALF, probes),
            root_columns.reshape(4, 2, HALF, probes),
        ),
    )
    table = lax.dynamic_index_in_dim(stacked, core, axis=1, keepdims=False)
    sent = jnp.sum(chosen[:, :, None, None] * table[:, None].astype(F32), axis=0).astype(BF16)
    ancestor = total(swap(sent, LEAF)).astype(BF16)
    leaf_back = row_scatter(backward(panel[None], ancestor[None])[0], core)
    leaf_reduced = (leaf_solved.astype(F32) - leaf_back).astype(BF16)
    leaf_solution = row_scatter(backward(inverse[None], leaf_reduced[None])[0], core).astype(BF16)

    own_rows = lax.dynamic_slice_in_dim(lower_columns, row * 16, 16, axis=1)
    by_separator = [own_rows[0]] + [shift(own_rows[step], "x", -step) for step in (1, 2, 3)]
    lower_solution = lax.dynamic_slice_in_dim(jnp.stack(by_separator + by_separator), (4 - x) % 4, 4, axis=0)
    middle_solution = lax.dynamic_slice_in_dim(middle_columns, row * 32, 32, axis=1)
    root_solution = lax.dynamic_slice_in_dim(root_columns, row * 64, 64, axis=0)
    return (leaf_solution[None], lower_solution, middle_solution, root_solution)


def solution(mesh):
    fine = Mesh(mesh.devices.reshape(4, 8, 4, 2), ("x", "z", "y", "core"))
    every = LEAF + ROW
    return jax.shard_map(
        body,
        mesh=fine,
        in_specs=(
            P(LEAF, ROW, None),
            P(None, every, None),
            P(None, every, None),
            P(every, None),
            P(LEAF, ROW, None),
            P(None, ROW, LEAF),
            P(None, ROW, LEAF),
            P(ROW, LEAF),
            P(LEAF, ROW, None),
            P(None, LEAF, ROW),
            P(None, LEAF, ROW),
            P(None, LEAF, ROW),
            P(),
            P(),
        ),
        out_specs=(
            P(LEAF, ROW, None),
            P(None, every, None),
            P(None, every, None),
            P(every, None),
        ),
        check_vma=False,
    )
```

profile of v0, /device:TPU:32, one launch (start us, length us, event | category | flops | bytes accessed | tf_op | source)
XLA Modules:
  0.0 408.0 jit_solution(12197404930608293247)
XLA Ops:
  2.7 10.9 %all_to_all.85 = bf16[4,256,128]{2,1,0:T(8,128)(2,1)S(1)} all-to-all(bf16[4,256,128]{2,1,0:T(8,128)(2,1)S(1)} %broadcast_in_dim.180), channel_id=1, replica_groups=mesh['x'=4,'z'=8,'y'=4,'core'=2] {'y'}, dimensions={0} | all-to-all | bytes 524288 | tf_op jit(solution)/shard_map/all_to_all | solution.py:18
  16.5 9.6 %all_to_all.86 = bf16[4,256,128]{2,1,0:T(8,128)(2,1)S(1)} all-to-all(bf16[4,256,128]{2,1,0:T(8,128)(2,1)S(1)} %broadcast_in_dim.182), channel_id=1, replica_groups=mesh['x'=4,'z'=8,'y'=4,'core'=2] {'y'}, dimensions={0} | all-to-all | bytes 524288 | tf_op jit(solution)/shard_map/all_to_all | solution.py:18
  29.3 11.2 %all-to-all-start.2 = ((bf16[32,64,128]{2,1,0:T(8,128)(2,1)}), bf16[32,64,128]{2,1,0:T(8,128)(2,1)S(1)}, u32[]{:S(2)}, u32[]{:S(2)}) async-start(bf16[32,64,128]{2,1,0:T(8,128)(2,1)} %pieces_product.3), calls=%async_computation.2 | async-start | bytes 1048576 | tf_op jit(solution)/shard_map/all_to_all | solution.py:18
  49.7 5.2 %collective-permute-done.1 = bf16[528,128]{1,0:T(8,128)(2,1)S(1)} collective-permute-done((bf16[528,128]{1,0:T(8,128)(2,1)S(1)}, bf16[528,128]{1,0:T(8,128)(2,1)S(1)}, u32[]{:S(2)}, u32[]{:S(2)}) %collective-permute-start.1) | collective-permute-done | bytes 135200 | tf_op jit(solution)/shard_map/ppermute | solution.py:46
  54.9 3.5 all-to-all-done.2
  59.8 3.5 all-to-all-start.3
  63.4 6.9 %all-to-all-done.3 = bf16[4,320,128]{2,1,0:T(8,128)(2,1)S(1)} async-done(((bf16[4,320,128]{2,1,0:T(8,128)(2,1)}), bf16[4,320,128]{2,1,0:T(8,128)(2,1)S(1)}, u32[]{:S(2)}, u32[]{:S(2)}) %all-to-all-start.3) | async-done | bytes 327712 | tf_op jit(solution)/shard_map/all_to_all | solution.py:18
  72.7 12.5 %all_to_all.87 = bf16[8,64,128]{2,1,0:T(8,128)(2,1)S(1)} all-to-all(bf16[8,64,128]{2,1,0:T(8,128)(2,1)S(1)} %bitcast.165), channel_id=1, replica_groups=mesh['x'=4,'z'=8,'y'=4,'core'=2] {'z'}, dimensions={0} | all-to-all | bytes 262144 | tf_op jit(solution)/shard_map/all_to_all | solution.py:18
  86.2 5.0 %all-to-all-start.5 = ((bf16[32,64,128]{2,1,0:T(8,128)(2,1)}), bf16[32,64,128]{2,1,0:T(8,128)(2,1)S(1)}, u32[]{:S(2)}, u32[]{:S(2)}) async-start(bf16[32,64,128]{2,1,0:T(8,128)(2,1)} %broadcast_in_dim.185), calls=%async_computation.5 | async-start | bytes 1048576 | tf_op jit(solution)/shard_map/all_to_all | solution.py:18
  93.2 14.9 %all-to-all-done.5 = bf16[32,64,128]{2,1,0:T(8,128)(2,1)S(1)} async-done(((bf16[32,64,128]{2,1,0:T(8,128)(2,1)}), bf16[32,64,128]{2,1,0:T(8,128)(2,1)S(1)}, u32[]{:S(2)}, u32[]{:S(2)}) %all-to-all-start.5) | async-done | bytes 524320 | tf_op jit(solution)/shard_map/all_to_all | solution.py:18
  122.3 22.8 %all_to_all.88 = bf16[32,64,128]{2,1,0:T(8,128)(2,1)} all-to-all(bf16[32,64,128]{2,1,0:T(8,128)(2,1)S(1)} %bitcast.155), channel_id=1, replica_groups=mesh['x'=4,'z'=8,'y'=4,'core'=2] {'x','z'}, dimensions={0} | all-to-all | bytes 1048576 | tf_op jit(solution)/shard_map/all_to_all | solution.py:18
  147.2 4.9 %all-to-all-start.7 = ((bf16[32,64,128]{2,1,0:T(8,128)(2,1)}), bf16[32,64,128]{2,1,0:T(8,128)(2,1)}, u32[]{:S(2)}, u32[]{:S(2)}) async-start(bf16[32,64,128]{2,1,0:T(8,128)(2,1)} %broadcast_in_dim.197), calls=%async_computation.7 | async-start | bytes 1048576 | tf_op jit(solution)/shard_map/all_to_all | solution.py:18
  155.6 13.9 %all-to-all-done.7 = bf16[32,64,128]{2,1,0:T(8,128)(2,1)} async-done(((bf16[32,64,128]{2,1,0:T(8,128)(2,1)}), bf16[32,64,128]{2,1,0:T(8,128)(2,1)}, u32[]{:S(2)}, u32[]{:S(2)}) %all-to-all-start.7) | async-done | bytes 524320 | tf_op jit(solution)/shard_map/all_to_all | solution.py:18
  187.5 22.7 %all_to_all.89 = bf16[32,64,128]{2,1,0:T(8,128)(2,1)} all-to-all(bf16[32,64,128]{2,1,0:T(8,128)(2,1)S(1)} %bitcast.157), channel_id=1, replica_groups=mesh['x'=4,'z'=8,'y'=4,'core'=2] {'x','z'}, dimensions={0} | all-to-all | bytes 1048576 | tf_op jit(solution)/shard_map/all_to_all | solution.py:18
  211.4 22.1 %all_to_all.90 = bf16[32,64,128]{2,1,0:T(8,128)(2,1)S(1)} all-to-all(bf16[32,64,128]{2,1,0:T(8,128)(2,1)S(1)} %broadcast_in_dim.209), channel_id=1, replica_groups=mesh['x'=4,'z'=8,'y'=4,'core'=2] {'x','z'}, dimensions={0} | all-to-all | bytes 1048576 | tf_op jit(solution)/shard_map/all_to_all | solution.py:18
  248.6 5.0 %all-to-all-start.10 = ((bf16[32,64,128]{2,1,0:T(8,128)(2,1)}), bf16[32,64,128]{2,1,0:T(8,128)(2,1)S(1)}, u32[]{:S(2)}, u32[]{:S(2)}) async-start(bf16[32,64,128]{2,1,0:T(8,128)(2,1)} %bitcast.34), calls=%async_computation.10 | async-start | bytes 1048576 | tf_op jit(solution)/shard_map/all_to_all | solution.py:18
  253.6 18.0 %all-to-all-done.10 = bf16[32,64,128]{2,1,0:T(8,128)(2,1)S(1)} async-done(((bf16[32,64,128]{2,1,0:T(8,128)(2,1)}), bf16[32,64,128]{2,1,0:T(8,128)(2,1)S(1)}, u32[]{:S(2)}, u32[]{:S(2)}) %all-to-all-start.10) | async-done | bytes 524320 | tf_op jit(solution)/shard_map/all_to_all | solution.py:18
  272.5 22.3 %all_to_all.91 = bf16[32,64,128]{2,1,0:T(8,128)(2,1)S(1)} all-to-all(bf16[32,64,128]{2,1,0:T(8,128)(2,1)S(1)} %broadcast_in_dim.213), channel_id=1, replica_groups=mesh['x'=4,'z'=8,'y'=4,'core'=2] {'x','z'}, dimensions={0} | all-to-all | bytes 1048576 | tf_op jit(solution)/shard_map/all_to_all | solution.py:18
  308.9 22.6 %all_to_all.92 = bf16[32,64,128]{2,1,0:T(8,128)(2,1)S(1)} all-to-all(bf16[32,64,128]{2,1,0:T(8,128)(2,1)S(1)} %bitcast.153), channel_id=1, replica_groups=mesh['x'=4,'z'=8,'y'=4,'core'=2] {'x','z'}, dimensions={0} | all-to-all | bytes 1048576 | tf_op jit(solution)/shard_map/all_to_all | solution.py:18
  331.6 11.3 %all_to_all.93 = bf16[8,64,128]{2,1,0:T(8,128)(2,1)S(1)} all-to-all(bf16[8,64,128]{2,1,0:T(8,128)(2,1)S(1)} %broadcast_in_dim.215), channel_id=1, replica_groups=mesh['x'=4,'z'=8,'y'=4,'core'=2] {'z'}, dimensions={0} | all-to-all | bytes 262144 | tf_op jit(solution)/shard_map/all_to_all | solution.py:18
  356.6 5.2 %all-to-all-start.14 = ((bf16[32,64,128]{2,1,0:T(8,128)(2,1)}), bf16[32,64,128]{2,1,0:T(8,128)(2,1)S(1)}, u32[]{:S(2)}, u32[]{:S(2)}) async-start(bf16[32,64,128]{2,1,0:T(8,128)(2,1)} %multiply_reduce_fusion), calls=%async_computation.14 | async-start | bytes 1048576 | tf_op jit(solution)/shard_map/all_to_all | solution.py:18
  367.6 12.6 %all-to-all-done.14 = bf16[32,64,128]{2,1,0:T(8,128)(2,1)S(1)} async-done(((bf16[32,64,128]{2,1,0:T(8,128)(2,1)}), bf16[32,64,128]{2,1,0:T(8,128)(2,1)S(1)}, u32[]{:S(2)}, u32[]{:S(2)}) %all-to-all-start.14) | async-done | bytes 524320 | tf_op jit(solution)/shard_map/all_to_all | solution.py:18
  386.6 7.2 %all-to-all-done.15 = bf16[4,256,128]{2,1,0:T(8,128)(2,1)S(1)} async-done(((bf16[4,256,128]{2,1,0:T(8,128)(2,1)}), bf16[4,256,128]{2,1,0:T(8,128)(2,1)S(1)}, u32[]{:S(2)}, u32[]{:S(2)}) %all-to-all-start.15) | async-done | bytes 262176 | tf_op jit(solution)/shard_map/all_to_all | solution.py:18
  400.8 6.6 %all-to-all-done.16 = bf16[4,256,128]{2,1,0:T(8,128)(2,1)S(1)} async-done(((bf16[4,256,128]{2,1,0:T(8,128)(2,1)}), bf16[4,256,128]{2,1,0:T(8,128)(2,1)S(1)}, u32[]{:S(2)}, u32[]{:S(2)}) %all-to-all-start.16) | async-done | bytes 262176 | tf_op jit(solution)/shard_map/all_to_all | solution.py:18
  (206 shorter events, 126.2 us)
Async XLA Ops:
  29.3 29.1 %all-to-all-start.2 = ((bf16[32,64,128]{2,1,0:T(8,128)(2,1)}), bf16[32,64,128]{2,1,0:T(8,128)(2,1)S(1)}, u32[]{:S(2)}, u32[]{:S(2)}) async-start(bf16[32,64,128]{2,1,0:T(8,128)(2,1)} %pieces_product.3), calls=%async_computation.2 | async-start | bytes 1048576 | tf_op jit(solution)/shard_map/all_to_all | solution.py:18
  40.5 9.2 %collective-permute-start = (bf16[528,128]{1,0:T(8,128)(2,1)S(1)}, bf16[528,128]{1,0:T(8,128)(2,1)S(1)}, u32[]{:S(2)}, u32[]{:S(2)}) collective-permute-start(bf16[528,128]{1,0:T(8,128)(2,1)S(1)} %get-tuple-element.16), channel_id=1, source_target_pairs={{0,64},{64,128},{128,192},{192,0},{1,65},{65,129},{129,193},{193,1... | collective-permute-start | bytes 405512 | tf_op jit(solution)/shard_map/ppermute | solution.py:46
  42.1 12.9 %collective-permute-start.1 = (bf16[528,128]{1,0:T(8,128)(2,1)S(1)}, bf16[528,128]{1,0:T(8,128)(2,1)S(1)}, u32[]{:S(2)}, u32[]{:S(2)}) collective-permute-start(bf16[528,128]{1,0:T(8,128)(2,1)S(1)} %get-tuple-element.17), channel_id=1, source_target_pairs={{0,128},{64,192},{128,0},{192,64},{1,129},{65,193},{129,1},{193,65... | collective-permute-start | bytes 405512 | tf_op jit(solution)/shard_map/ppermute | solution.py:46
  44.8 10.1 %collective-permute-start.2 = (bf16[528,128]{1,0:T(8,128)(2,1)S(1)}, bf16[528,128]{1,0:T(8,128)(2,1)S(1)}, u32[]{:S(2)}, u32[]{:S(2)}) collective-permute-start(bf16[528,128]{1,0:T(8,128)(2,1)S(1)} %get-tuple-element.18), channel_id=1, source_target_pairs={{0,192},{64,0},{128,64},{192,128},{1,193},{65,1},{129,65},{193,129... | collective-permute-start | bytes 405512 | tf_op jit(solution)/shard_map/ppermute | solution.py:46
  59.8 10.5 %all-to-all-start.3 = ((bf16[4,320,128]{2,1,0:T(8,128)(2,1)}), bf16[4,320,128]{2,1,0:T(8,128)(2,1)S(1)}, u32[]{:S(2)}, u32[]{:S(2)}) async-start(bf16[4,320,128]{2,1,0:T(8,128)(2,1)} %broadcast_in_dim.184), calls=%async_computation.3 | async-start | bytes 655360 | tf_op jit(solution)/shard_map/all_to_all | solution.py:18
  86.2 21.9 %all-to-all-start.5 = ((bf16[32,64,128]{2,1,0:T(8,128)(2,1)}), bf16[32,64,128]{2,1,0:T(8,128)(2,1)S(1)}, u32[]{:S(2)}, u32[]{:S(2)}) async-start(bf16[32,64,128]{2,1,0:T(8,128)(2,1)} %broadcast_in_dim.185), calls=%async_computation.5 | async-start | bytes 1048576 | tf_op jit(solution)/shard_map/all_to_all | solution.py:18
  112.0 6.8 %collective-permute-start.3 = (bf16[256,128]{1,0:T(8,128)(2,1)S(1)}, bf16[256,128]{1,0:T(8,128)(2,1)S(1)}, u32[]{:S(2)}, u32[]{:S(2)}) collective-permute-start(bf16[256,128]{1,0:T(8,128)(2,1)S(1)} %dynamic-slice_reduce_fusion.4), channel_id=1, source_target_pairs={{0,2},{2,4},{4,6},{6,0},{1,3},{3,5},{5,7},{7,1},{8,10},{10,12},{12... | collective-permute-start | bytes 196616 | tf_op jit(solution)/shard_map/ppermute | solution.py:46
  112.6 6.2 %collective-permute-start.4 = (bf16[256,128]{1,0:T(8,128)(2,1)S(1)}, bf16[256,128]{1,0:T(8,128)(2,1)S(1)}, u32[]{:S(2)}, u32[]{:S(2)}) collective-permute-start(bf16[256,128]{1,0:T(8,128)(2,1)S(1)} %dynamic-slice_reduce_fusion.4), channel_id=1, source_target_pairs={{0,4},{2,6},{4,0},{6,2},{1,5},{3,7},{5,1},{7,3},{8,12},{10,14},{12... | collective-permute-start | bytes 196616 | tf_op jit(solution)/shard_map/ppermute | solution.py:46
  147.2 22.4 %all-to-all-start.7 = ((bf16[32,64,128]{2,1,0:T(8,128)(2,1)}), bf16[32,64,128]{2,1,0:T(8,128)(2,1)}, u32[]{:S(2)}, u32[]{:S(2)}) async-start(bf16[32,64,128]{2,1,0:T(8,128)(2,1)} %broadcast_in_dim.197), calls=%async_computation.7 | async-start | bytes 1048576 | tf_op jit(solution)/shard_map/all_to_all | solution.py:18
  176.0 5.7 %collective-permute-start.6 = (bf16[256,128]{1,0:T(8,128)(2,1)S(1)}, bf16[256,128]{1,0:T(8,128)(2,1)S(1)}, u32[]{:S(2)}, u32[]{:S(2)}) collective-permute-start(bf16[256,128]{1,0:T(8,128)(2,1)S(1)} %dynamic-slice_reduce_fusion.3), channel_id=1, source_target_pairs={{0,2},{2,4},{4,6},{6,0},{1,3},{3,5},{5,7},{7,1},{8,10},{10,12},{12... | collective-permute-start | bytes 196616 | tf_op jit(solution)/shard_map/ppermute | solution.py:46
  177.1 6.5 %collective-permute-start.7 = (bf16[256,128]{1,0:T(8,128)(2,1)S(1)}, bf16[256,128]{1,0:T(8,128)(2,1)S(1)}, u32[]{:S(2)}, u32[]{:S(2)}) collective-permute-start(bf16[256,128]{1,0:T(8,128)(2,1)S(1)} %dynamic-slice_reduce_fusion.3), channel_id=1, source_target_pairs={{0,4},{2,6},{4,0},{6,2},{1,5},{3,7},{5,1},{7,3},{8,12},{10,14},{12... | collective-permute-start | bytes 196616 | tf_op jit(solution)/shard_map/ppermute | solution.py:46
  236.7 6.0 %collective-permute-start.10 = (bf16[256,128]{1,0:T(8,128)(2,1)S(1)}, bf16[256,128]{1,0:T(8,128)(2,1)S(1)}, u32[]{:S(2)}, u32[]{:S(2)}) collective-permute-start(bf16[256,128]{1,0:T(8,128)(2,1)S(1)} %dynamic-slice_reduce_fusion.2), channel_id=1, source_target_pairs={{0,4},{2,6},{4,0},{6,2},{1,5},{3,7},{5,1},{7,3},{8,12},{10,14},{12... | collective-permute-start | bytes 196616 | tf_op jit(solution)/shard_map/ppermute | solution.py:46
  239.6 5.5 %collective-permute-start.9 = (bf16[256,128]{1,0:T(8,128)(2,1)S(1)}, bf16[256,128]{1,0:T(8,128)(2,1)S(1)}, u32[]{:S(2)}, u32[]{:S(2)}) collective-permute-start(bf16[256,128]{1,0:T(8,128)(2,1)S(1)} %dynamic-slice_reduce_fusion.2), channel_id=1, source_target_pairs={{0,2},{2,4},{4,6},{6,0},{1,3},{3,5},{5,7},{7,1},{8,10},{10,12},{12... | collective-permute-start | bytes 196616 | tf_op jit(solution)/shard_map/ppermute | solution.py:46
  248.6 22.9 %all-to-all-start.10 = ((bf16[32,64,128]{2,1,0:T(8,128)(2,1)}), bf16[32,64,128]{2,1,0:T(8,128)(2,1)S(1)}, u32[]{:S(2)}, u32[]{:S(2)}) async-start(bf16[32,64,128]{2,1,0:T(8,128)(2,1)} %bitcast.34), calls=%async_computation.10 | async-start | bytes 1048576 | tf_op jit(solution)/shard_map/all_to_all | solution.py:18
  298.0 6.8 %collective-permute-start.12 = (bf16[256,128]{1,0:T(8,128)(2,1)S(1)}, bf16[256,128]{1,0:T(8,128)(2,1)S(1)}, u32[]{:S(2)}, u32[]{:S(2)}) collective-permute-start(bf16[256,128]{1,0:T(8,128)(2,1)S(1)} %dynamic-slice_reduce_fusion.1), channel_id=1, source_target_pairs={{0,2},{2,4},{4,6},{6,0},{1,3},{3,5},{5,7},{7,1},{8,10},{10,12},{12... | collective-permute-start | bytes 196616 | tf_op jit(solution)/shard_map/ppermute | solution.py:46
  298.1 6.8 %collective-permute-start.13 = (bf16[256,128]{1,0:T(8,128)(2,1)S(1)}, bf16[256,128]{1,0:T(8,128)(2,1)S(1)}, u32[]{:S(2)}, u32[]{:S(2)}) collective-permute-start(bf16[256,128]{1,0:T(8,128)(2,1)S(1)} %dynamic-slice_reduce_fusion.1), channel_id=1, source_target_pairs={{0,4},{2,6},{4,0},{6,2},{1,5},{3,7},{5,1},{7,3},{8,12},{10,14},{12... | collective-permute-start | bytes 196616 | tf_op jit(solution)/shard_map/ppermute | solution.py:46
  345.3 5.9 %collective-permute-start.15 = (bf16[256,128]{1,0:T(8,128)(2,1)S(1)}, bf16[256,128]{1,0:T(8,128)(2,1)S(1)}, u32[]{:S(2)}, u32[]{:S(2)}) collective-permute-start(bf16[256,128]{1,0:T(8,128)(2,1)S(1)} %dynamic-slice_reduce_fusion), channel_id=1, source_target_pairs={{0,2},{2,4},{4,6},{6,0},{1,3},{3,5},{5,7},{7,1},{8,10},{10,12},{12... | collective-permute-start | bytes 196616 | tf_op jit(solution)/shard_map/ppermute | solution.py:46
  346.4 6.3 %collective-permute-start.16 = (bf16[256,128]{1,0:T(8,128)(2,1)S(1)}, bf16[256,128]{1,0:T(8,128)(2,1)S(1)}, u32[]{:S(2)}, u32[]{:S(2)}) collective-permute-start(bf16[256,128]{1,0:T(8,128)(2,1)S(1)} %dynamic-slice_reduce_fusion), channel_id=1, source_target_pairs={{0,4},{2,6},{4,0},{6,2},{1,5},{3,7},{5,1},{7,3},{8,12},{10,14},{12... | collective-permute-start | bytes 196616 | tf_op jit(solution)/shard_map/ppermute | solution.py:46
  356.6 23.6 %all-to-all-start.14 = ((bf16[32,64,128]{2,1,0:T(8,128)(2,1)}), bf16[32,64,128]{2,1,0:T(8,128)(2,1)S(1)}, u32[]{:S(2)}, u32[]{:S(2)}) async-start(bf16[32,64,128]{2,1,0:T(8,128)(2,1)} %multiply_reduce_fusion), calls=%async_computation.14 | async-start | bytes 1048576 | tf_op jit(solution)/shard_map/all_to_all | solution.py:18
  363.1 17.7 %collective-permute-start.20 = (bf16[16,128]{1,0:T(8,128)(2,1)S(1)}, bf16[16,128]{1,0:T(8,128)(2,1)S(1)}, u32[]{:S(2)}, u32[]{:S(2)}) collective-permute-start(bf16[16,128]{1,0:T(8,128)(2,1)S(1)} %get-tuple-element.33), channel_id=1, source_target_pairs={{0,192},{64,0},{128,64},{192,128},{1,193},{65,1},{129,65},{193,129... | collective-permute-start | bytes 12296 | tf_op jit(solution)/shard_map/ppermute | solution.py:46
  366.0 14.9 %collective-permute-start.21 = (bf16[16,128]{1,0:T(8,128)(2,1)S(1)}, bf16[16,128]{1,0:T(8,128)(2,1)S(1)}, u32[]{:S(2)}, u32[]{:S(2)}) collective-permute-start(bf16[16,128]{1,0:T(8,128)(2,1)S(1)} %get-tuple-element.32), channel_id=1, source_target_pairs={{0,128},{64,192},{128,0},{192,64},{1,129},{65,193},{129,1},{193,65... | collective-permute-start | bytes 12296 | tf_op jit(solution)/shard_map/ppermute | solution.py:46
  366.7 19.9 %collective-permute-start.22 = (bf16[16,128]{1,0:T(8,128)(2,1)S(1)}, bf16[16,128]{1,0:T(8,128)(2,1)S(1)}, u32[]{:S(2)}, u32[]{:S(2)}) collective-permute-start(bf16[16,128]{1,0:T(8,128)(2,1)S(1)} %get-tuple-element.30), channel_id=1, source_target_pairs={{0,64},{64,128},{128,192},{192,0},{1,65},{65,129},{129,193},{193,1... | collective-permute-start | bytes 12296 | tf_op jit(solution)/shard_map/ppermute | solution.py:46
  383.1 10.6 %all-to-all-start.15 = ((bf16[4,256,128]{2,1,0:T(8,128)(2,1)}), bf16[4,256,128]{2,1,0:T(8,128)(2,1)S(1)}, u32[]{:S(2)}, u32[]{:S(2)}) async-start(bf16[4,256,128]{2,1,0:T(8,128)(2,1)} %fusion.1), calls=%async_computation.15 | async-start | bytes 524288 | tf_op jit(solution)/shard_map/all_to_all | solution.py:18
  396.7 10.6 %all-to-all-start.16 = ((bf16[4,256,128]{2,1,0:T(8,128)(2,1)}), bf16[4,256,128]{2,1,0:T(8,128)(2,1)S(1)}, u32[]{:S(2)}, u32[]{:S(2)}) async-start(bf16[4,256,128]{2,1,0:T(8,128)(2,1)} %fusion), calls=%async_computation.16 | async-start | bytes 524288 | tf_op jit(solution)/shard_map/all_to_all | solution.py:18
  (29 other events, 501.0 us)
where the time goes:
time: 410 us; the launch traced here: 408 us
  blocking collectives  183 us (45%)
  waiting for transfers between devices  116 us (28%)
  starting transfers between devices  70.3 us (17%)
  Pallas kernels  14.5 us (4%)
  local copies, waits for them, and re-layouts  12.6 us (3%)
  other arithmetic  10.6 us (3%)
    all_to_all x9, blocking collectives, swap(): return lax.all_to_all(pieces, axes, split_axis=0, concat_axis=0, tiled=True)  157 us
    all_to_all x8, waiting for transfers between devices, swap(): return lax.all_to_all(pieces, axes, split_axis=0, concat_axis=0, tiled=True)  83.5 us
    all_to_all x8, starting transfers between devices, swap(): return lax.all_to_all(pieces, axes, split_axis=0, concat_axis=0, tiled=True)  41.5 us
    ppermute x21, waiting for transfers between devices, shift(): return lax.ppermute(piece, axis, [(i, (i + step) % 4) for i in range(4)])  29.3 us
    ppermute x21, starting transfers between devices, shift(): return lax.ppermute(piece, axis, [(i, (i + step) % 4) for i in range(4)])  28.6 us
    all_gather x13, blocking collectives, both_cores(): return lax.all_gather(piece, 'core', axis=0, tiled=False)  25.9 us
  transfers between devices with their start and end apart: 31, of which 25 were waited for; matrix products, arithmetic and copies ran while one was open for 2% of the time, Pallas kernels for 0%

commit v1 on v0

--- a/solution.py
+++ b/solution.py
@@ -10,6 +10,7 @@
 LEAVES = 32
 ROWS = 8
 HALF = 64
+BLOCK = 128
 F32 = jnp.float32
 BF16 = jnp.bfloat16
 
@@ -34,6 +35,10 @@
     return swap(copies(piece.astype(BF16), LEAVES), LEAF)
 
 
+def cut(array, start, size, axis):
+    return lax.dynamic_slice_in_dim(array, start.astype(jnp.uint32), size, axis=axis)
+
+
 def z_terms(partial):
     return swap(partial.reshape(8, HALF, -1), "z")
 
@@ -46,6 +51,10 @@
     return lax.ppermute(piece, axis, [(i, (i + step) % 4) for i in range(4)])
 
 
+def take(array, index, axis):
+    return lax.dynamic_index_in_dim(array, index.astype(jnp.uint32), axis=axis, keepdims=False)
+
+
 def both_cores(piece):
     return lax.all_gather(piece, "core", axis=0, tiled=False)
 
@@ -54,11 +63,11 @@
     return both_cores(swap(copies(piece, 4), "y"))
 
 
-def row_half_sum(partial, core):
-    halves = lax.dynamic_slice_in_dim(both_cores(partial), core * 256, 256, axis=1)
-    pair = total(halves).astype(BF16)
+def row_half_sum(partial, core, beside=None):
+    pair = total(take(both_cores(partial.reshape(2, 256, -1)), core, 1)).astype(BF16)
     others = [shift(pair, "y", step) for step in (1, 2, 3)]
-    return sum([piece.astype(F32) for piece in others], pair.astype(F32))
+    result = sum([piece.astype(F32) for piece in others], pair.astype(F32))
+    return result if beside is None else (result, beside(pair))
 
 
 def row_scatter(partial, core):
@@ -98,38 +107,65 @@
     )(matrix, columns)
 
 
-def forward_total(matrix, columns, start, group, dtype):
+def forward_total(matrix, columns, position, landed, own_probes, carried, dtype):
     count, rows, depth = matrix.shape
     probes = columns.shape[-1]
-
-    def kernel(matrix_ref, columns_ref, start_ref, out_ref, sum_ref):
-        member = pl.program_id(0) % group
-
-        @pl.when(member == 0)
-        def _():
-            sum_ref[...] = start_ref[0]
-
-        sum_ref[...] += product(matrix_ref[0], columns_ref[0])
-
-        @pl.when(member == group - 1)
-        def _():
-            out_ref[0] = sum_ref[...].astype(dtype)
-
-    in_specs = [
-        pl.BlockSpec((1, rows, depth), lambda s: (s, 0, 0)),
-        pl.BlockSpec((1, depth, probes), lambda s: (s, 0, 0)),
-        pl.BlockSpec((1, rows, probes), lambda s: (s // group, 0, 0)),
+    groups = (own_probes if carried is None else carried).shape[0]
+    group = count // groups
+    slots = rows // BLOCK
+
+    parts = 2
+    part = rows // parts
+
+    def kernel(position_ref, matrix_ref, columns_ref, *refs):
+        out_ref, held_ref, sems, sum_ref = refs[-4:]
+        moves = {}
+        for member in range(count):
+            for piece in range(parts):
+                at = pl.ds(piece * part, part)
+                moves[member, piece] = pltpu.make_async_copy(
+                    matrix_ref.at[member, at], held_ref.at[member, at], sems.at[member * parts + piece]
+                )
+                moves[member, piece].start()
+        for unit in range(groups):
+            for piece in range(parts):
+                at = slice(piece * part, piece * part + part)
+                result = refs[0][unit, at].astype(F32) if carried is not None else jnp.zeros((part, probes), F32)
+                for member in range(unit * group, unit * group + group):
+                    moves[member, piece].wait()
+                    result += product(held_ref[member, at], columns_ref[member])
+                if carried is not None:
+                    out_ref[unit, at] = result.astype(dtype)
+                else:
+                    sum_ref[unit, at] = result
+            if carried is None:
+                landed_ref, own_ref = refs[:2]
+                here, core, row = position_ref[0], position_ref[1], position_ref[2]
+                for slot in range(slots):
+                    at = pl.ds(pl.multiple_of(slot * BLOCK + core * HALF, HALF), HALF)
+                    sum_ref[unit, at, :] += jnp.where(here > 0, landed_ref[unit * slots + slot].astype(F32), 0.0)
+                own = rows // ROWS
+                at = pl.ds(pl.multiple_of(row * own, own), own)
+                sum_ref[unit, at, :] -= own_ref[unit].astype(F32)
+                out_ref[unit] = sum_ref[unit].astype(dtype)
+
+    vmem = pl.BlockSpec(memory_space=pltpu.VMEM)
+    operands = (landed, own_probes) if carried is None else (carried,)
+    scratch = [
+        pltpu.VMEM((count, rows, depth), BF16),
+        pltpu.SemaphoreType.DMA((count * parts,)),
+        pltpu.VMEM((groups, rows, probes), F32),
     ]
     return pl.pallas_call(
         kernel,
-        out_shape=jax.ShapeDtypeStruct((count // group, rows, probes), dtype),
-        grid=(count,),
-        in_specs=in_specs,
-        out_specs=pl.BlockSpec((1, rows, probes), lambda s: (s // group, 0, 0)),
-        scratch_shapes=[pltpu.VMEM((rows, probes), F32)],
+        out_shape=jax.ShapeDtypeStruct((groups, rows, probes), dtype),
+        in_specs=[pl.BlockSpec(memory_space=pltpu.SMEM), pl.BlockSpec(memory_space=pltpu.HBM), vmem]
+        + [vmem] * len(operands),
+        out_specs=vmem,
+        scratch_shapes=scratch,
         compiler_params=LIMITS,
         name="forward_total",
-    )(matrix, columns, start)
+    )(position, pltpu.with_memory_space_constraint(matrix, pltpu.HBM), columns, *operands)
 
 
 def backward(matrix, rows_in, depth_at_once=512):
@@ -244,12 +280,7 @@
     inverse = leaf_inverse[0]
     panel = leaf_panel[0]
 
-    lower_held = jnp.concatenate([lower_inverse, lower_probes], axis=1)
-    leaving = [lax.dynamic_index_in_dim(lower_held, (x + step) % 4, axis=0, keepdims=False) for step in range(4)]
-    leaf_probes, leaving = lax.optimization_barrier((leaf_probes, leaving))
-    lower_tiles = [leaving[0]] + [shift(leaving[step], "x", step) for step in (1, 2, 3)]
-
-    block = lax.dynamic_index_in_dim(leaf_blocks, y, axis=1, keepdims=False)
+    block = take(leaf_blocks, y, 1)
     parent = leaf_parent
     slot = jnp.where(
         y < 2,
@@ -265,6 +296,10 @@
     held = row_gather(leaf_probes[0])
     leaf_solved = pieces_product(inverse, held, 1)[0]
     updates = pieces_product(panel, row_gather(leaf_solved), LEAVES)
+    updates, tiles, pieces = lax.optimization_barrier((updates, lower_inverse, lower_probes))
+    lower_held = jnp.concatenate([tiles, pieces], axis=1)
+    leaving = [take(lower_held, (x + step) % 4, 0) for step in range(4)]
+    lower_tiles = [leaving[0]] + [shift(leaving[step], "x", step) for step in (1, 2, 3)]
     received, lower_tiles = lax.optimization_barrier((swap(updates, LEAF), lower_tiles))
     lower_square = jnp.concatenate([tile[:512] for tile in lower_tiles], axis=1)[None]
     lower_pieces = jnp.concatenate([tile[512:] for tile in lower_tiles])
@@ -278,30 +313,28 @@
     lower_own = by_half[:, 4:].reshape(2, 4, 4, 16, probes).transpose(2, 1, 0, 3, 4).reshape(4, 128, probes)
     lower_input = (lower_own.astype(F32) - lower_added.astype(F32)).astype(BF16).reshape(1, 512, probes)
 
-    half_ids = lax.broadcasted_iota(jnp.int32, (1, 2, 1, 1), 1)
-    row_ids = lax.broadcasted_iota(jnp.int32, (1, ROWS, 1, 1), 1)
-
-    def contribution(level, own_probes):
-        placed = jnp.where((half_ids == core) & (y == level), landed[:, None].astype(F32), 0.0)
-        own = jnp.where(row_ids == row, own_probes[:, None].astype(F32), 0.0)
-        return placed.reshape(own_probes.shape[0], -1, probes) - own.reshape(own_probes.shape[0], -1, probes)
-
-    middle_start = contribution(2, middle_probes)
-    root_start = contribution(3, root_probes[None])
-
     lower_terms = z_terms(forward(lower_square, lower_input))
     lower_gathered = leaf_gather(total(lower_terms))
-    lower_solved = lax.dynamic_index_in_dim(lower_gathered, leaf, axis=0, keepdims=False)
+    lower_solved = take(lower_gathered, leaf, 0)
     lower_block = lower_gathered.reshape(4, 512, probes)
-    to_middle = forward_total(lower_to_middle, lower_block, middle_start, 2, BF16).reshape(512, probes)
-    middle_input = both_cores((-row_half_sum(to_middle, core)).astype(BF16))
-    to_root = forward_total(lower_to_root, lower_block, root_start, 4, F32)
+
+    def at_level(level):
+        return jnp.stack([(y == level).astype(jnp.int32), core, row])
+
+    def early_root(pair):
+        block, _ = lax.optimization_barrier((lower_block, pair))
+        return forward_total(lower_to_root, block, at_level(3), landed, root_probes[None], None, F32)
+
+    to_middle = forward_total(lower_to_middle, lower_block, at_level(2), landed, middle_probes, None, BF16).reshape(512, probes)
+    middle_half, to_root = row_half_sum(to_middle, core, early_root)
+    middle_half, to_root = lax.optimization_barrier((middle_half, to_root))
+    middle_input = both_cores((-middle_half).astype(BF16))
 
     middle_terms = leaf_terms(forward(middle_inverse, middle_input))
     middle_gathered = leaf_gather(total(middle_terms))
-    middle_solved = lax.dynamic_index_in_dim(middle_gathered, leaf, axis=0, keepdims=False)
+    middle_solved = take(middle_gathered, leaf, 0)
     middle_block = middle_gathered.reshape(2, 1024, probes)
-    to_root = forward_total(middle_to_root, middle_block, to_root, 2, BF16).reshape(512, probes)
+    to_root = forward_total(middle_to_root, middle_block, at_level(3), None, None, to_root, BF16).reshape(512, probes)
     root_input = both_cores((-row_half_sum(to_root, core)).astype(BF16)).reshape(1, 512, probes)
 
     root_terms = leaf_terms(forward(root_inverse[None], root_input))
@@ -328,18 +361,18 @@
             root_columns.reshape(4, 2, HALF, probes),
         ),
     )
-    table = lax.dynamic_index_in_dim(stacked, core, axis=1, keepdims=False)
+    table = take(stacked, core, 1)
     sent = jnp.sum(chosen[:, :, None, None] * table[:, None].astype(F32), axis=0).astype(BF16)
     ancestor = total(swap(sent, LEAF)).astype(BF16)
     leaf_back = row_scatter(backward(panel[None], ancestor[None])[0], core)
     leaf_reduced = (leaf_solved.astype(F32) - leaf_back).astype(BF16)
     leaf_solution = row_scatter(backward(inverse[None], leaf_reduced[None])[0], core).astype(BF16)
 
-    own_rows = lax.dynamic_slice_in_dim(lower_columns, row * 16, 16, axis=1)
+    own_rows = cut(lower_columns, row * 16, 16, 1)
     by_separator = [own_rows[0]] + [shift(own_rows[step], "x", -step) for step in (1, 2, 3)]
-    lower_solution = lax.dynamic_slice_in_dim(jnp.stack(by_separator + by_separator), (4 - x) % 4, 4, axis=0)
-    middle_solution = lax.dynamic_slice_in_dim(middle_columns, row * 32, 32, axis=1)
-    root_solution = lax.dynamic_slice_in_dim(root_columns, row * 64, 64, axis=0)
+    lower_solution = cut(jnp.stack(by_separator + by_separator), (4 - x) % 4, 4, 0)
+    middle_solution = cut(middle_columns, row * 32, 32, 1)
+    root_solution = cut(root_columns, row * 64, 64, 0)
     return (leaf_solution[None], lower_solution, middle_solution, root_solution)
 
 

time: 410 us -> 409 us (level)
  blocking collectives: 183 us -> 205 us
  waiting for transfers between devices: 116 us -> 100 us
  local copies, waits for them, and re-layouts: 12.6 us -> 7.04 us
  Pallas kernels: 14.5 us -> 19.1 us
    all_to_all x9 -> x10, blocking collectives: 157 us -> 179 us  [swap(): return lax.all_to_all(pieces, axes, split_axis=0, concat_axis=0, tiled=True)]
    all_to_all x8 -> x7, waiting for transfers between devices: 83.5 us -> 71.1 us  [swap(): return lax.all_to_all(pieces, axes, split_axis=0, concat_axis=0, tiled=True)]
    pallas_call x3, Pallas kernels: 4.1 us -> 8.66 us  [forward_total(): pl.pallas_call(kernel, out_shape=jax.ShapeDtypeStruct((groups, rows, prob...]
    unnamed x55 -> x49, local copies, waits for them, and re-layouts: 6.25 us -> 1.97 us
    all_to_all x8 -> x7, starting transfers between devices: 41.5 us -> 37.3 us  [swap(): return lax.all_to_all(pieces, axes, split_axis=0, concat_axis=0, tiled=True)]
  transfers between devices with their start and end apart: 31 -> 30, of which waited for: 25 -> 24; matrix products, arithmetic and copies ran while one was open for 2% -> 1% of each run, Pallas kernels for 0% -> 1%
where the time goes in v1:
time: 409 us; the launch traced here: 407 us
  blocking collectives  205 us (50%)
  waiting for transfers between devices  100 us (24%)
  starting transfers between devices  67 us (16%)
  Pallas kernels  19.1 us (5%)
  other arithmetic  7.67 us (2%)
  local copies, waits for them, and re-layouts  7.04 us (2%)
    all_to_all x10, blocking collectives, swap(): return lax.all_to_all(pieces, axes, split_axis=0, concat_axis=0, tiled=True)  179 us
    all_to_all x7, waiting for transfers between devices, swap(): return lax.all_to_all(pieces, axes, split_axis=0, concat_axis=0, tiled=True)  71.1 us
    all_to_all x7, starting transfers between devices, swap(): return lax.all_to_all(pieces, axes, split_axis=0, concat_axis=0, tiled=True)  37.3 us
    ppermute x21, starting transfers between devices, shift(): return lax.ppermute(piece, axis, [(i, (i + step) % 4) for i in range(4)])  29.6 us
    all_gather x13, blocking collectives, both_cores(): return lax.all_gather(piece, 'core', axis=0, tiled=False)  26.2 us
    ppermute x21, waiting for transfers between devices, shift(): return lax.ppermute(piece, axis, [(i, (i + step) % 4) for i in range(4)])  26 us
    pallas_call x3, Pallas kernels, forward_total(): pl.pallas_call(kernel, out_shape=jax.ShapeDtypeStruct((groups, rows, prob...  8.66 us
  transfers between devices with their start and end apart: 30, of which 24 were waited for; matrix products, arithmetic and copies ran while one was open for 1% of the time, Pallas kernels for 1%

profile of v1, /device:TPU:32, one launch (start us, length us, event | category | flops | bytes accessed | tf_op | source)
XLA Modules:
  0.0 407.0 jit_solution(4083110004705254260)
XLA Ops:
  1.6 10.9 %all_to_all.85 = bf16[4,256,128]{2,1,0:T(8,128)(2,1)S(1)} all-to-all(bf16[4,256,128]{2,1,0:T(8,128)(2,1)S(1)} %broadcast_in_dim.43), channel_id=1, replica_groups=mesh['x'=4,'z'=8,'y'=4,'core'=2] {'y'}, dimensions={0} | all-to-all | bytes 524288 | tf_op jit(solution)/shard_map/all_to_all | solution.py:19
  15.9 9.6 %all_to_all.86 = bf16[4,256,128]{2,1,0:T(8,128)(2,1)S(1)} all-to-all(bf16[4,256,128]{2,1,0:T(8,128)(2,1)S(1)} %broadcast_in_dim.45), channel_id=1, replica_groups=mesh['x'=4,'z'=8,'y'=4,'core'=2] {'y'}, dimensions={0} | all-to-all | bytes 524288 | tf_op jit(solution)/shard_map/all_to_all | solution.py:19
  28.9 11.2 %all-to-all-start.2 = ((bf16[32,64,128]{2,1,0:T(8,128)(2,1)}), bf16[32,64,128]{2,1,0:T(8,128)(2,1)S(1)}, u32[]{:S(2)}, u32[]{:S(2)}) async-start(bf16[32,64,128]{2,1,0:T(8,128)(2,1)} %pieces_product.3), calls=%async_computation.2 | async-start | bytes 1048576 | tf_op jit(solution)/shard_map/all_to_all | solution.py:19
  46.7 4.4 %collective-permute-done = bf16[528,128]{1,0:T(8,128)(2,1)S(1)} collective-permute-done((bf16[528,128]{1,0:T(8,128)(2,1)S(1)}, bf16[528,128]{1,0:T(8,128)(2,1)S(1)}, u32[]{:S(2)}, u32[]{:S(2)}) %collective-permute-start) | collective-permute-done | bytes 135200 | tf_op jit(solution)/shard_map/ppermute | solution.py:51
  51.1 3.8 collective-permute-done.1
  59.4 3.5 all-to-all-start.3
  63.0 6.9 %all-to-all-done.3 = bf16[4,320,128]{2,1,0:T(8,128)(2,1)S(1)} async-done(((bf16[4,320,128]{2,1,0:T(8,128)(2,1)}), bf16[4,320,128]{2,1,0:T(8,128)(2,1)S(1)}, u32[]{:S(2)}, u32[]{:S(2)}) %all-to-all-start.3) | async-done | bytes 327712 | tf_op jit(solution)/shard_map/all_to_all | solution.py:19
  72.3 12.3 %all_to_all.87 = bf16[8,64,128]{2,1,0:T(8,128)(2,1)S(1)} all-to-all(bf16[8,64,128]{2,1,0:T(8,128)(2,1)S(1)} %bitcast.166), channel_id=1, replica_groups=mesh['x'=4,'z'=8,'y'=4,'core'=2] {'z'}, dimensions={0} | all-to-all | bytes 262144 | tf_op jit(solution)/shard_map/all_to_all | solution.py:19
  85.5 5.8 %all-to-all-start.5 = ((bf16[32,64,128]{2,1,0:T(8,128)(2,1)}), bf16[32,64,128]{2,1,0:T(8,128)(2,1)S(1)}, u32[]{:S(2)}, u32[]{:S(2)}) async-start(bf16[32,64,128]{2,1,0:T(8,128)(2,1)} %broadcast_in_dim.94), calls=%async_computation.5 | async-start | bytes 1048576 | tf_op jit(solution)/shard_map/all_to_all | solution.py:19
  91.5 16.9 %all-to-all-done.5 = bf16[32,64,128]{2,1,0:T(8,128)(2,1)S(1)} async-done(((bf16[32,64,128]{2,1,0:T(8,128)(2,1)}), bf16[32,64,128]{2,1,0:T(8,128)(2,1)S(1)}, u32[]{:S(2)}, u32[]{:S(2)}) %all-to-all-start.5) | async-done | bytes 524320 | tf_op jit(solution)/shard_map/all_to_all | solution.py:19
  123.5 22.6 %all_to_all.88 = bf16[32,64,128]{2,1,0:T(8,128)(2,1)S(1)} all-to-all(bf16[32,64,128]{2,1,0:T(8,128)(2,1)S(1)} %bitcast.153), channel_id=1, replica_groups=mesh['x'=4,'z'=8,'y'=4,'core'=2] {'x','z'}, dimensions={0} | all-to-all | bytes 1048576 | tf_op jit(solution)/shard_map/all_to_all | solution.py:19
  146.4 22.1 %all_to_all.89 = bf16[32,64,128]{2,1,0:T(8,128)(2,1)S(1)} all-to-all(bf16[32,64,128]{2,1,0:T(8,128)(2,1)S(1)} %broadcast_in_dim.96), channel_id=1, replica_groups=mesh['x'=4,'z'=8,'y'=4,'core'=2] {'x','z'}, dimensions={0} | all-to-all | bytes 1048576 | tf_op jit(solution)/shard_map/all_to_all | solution.py:19
  186.1 22.7 %all_to_all.90 = bf16[32,64,128]{2,1,0:T(8,128)(2,1)} all-to-all(bf16[32,64,128]{2,1,0:T(8,128)(2,1)S(1)} %bitcast.155), channel_id=1, replica_groups=mesh['x'=4,'z'=8,'y'=4,'core'=2] {'x','z'}, dimensions={0} | all-to-all | bytes 1048576 | tf_op jit(solution)/shard_map/all_to_all | solution.py:19
  210.1 22.1 %all_to_all.91 = bf16[32,64,128]{2,1,0:T(8,128)(2,1)S(1)} all-to-all(bf16[32,64,128]{2,1,0:T(8,128)(2,1)S(1)} %broadcast_in_dim.98), channel_id=1, replica_groups=mesh['x'=4,'z'=8,'y'=4,'core'=2] {'x','z'}, dimensions={0} | all-to-all | bytes 1048576 | tf_op jit(solution)/shard_map/all_to_all | solution.py:19
  247.8 5.0 %all-to-all-start.10 = ((bf16[32,64,128]{2,1,0:T(8,128)(2,1)}), bf16[32,64,128]{2,1,0:T(8,128)(2,1)S(1)}, u32[]{:S(2)}, u32[]{:S(2)}) async-start(bf16[32,64,128]{2,1,0:T(8,128)(2,1)} %bitcast.37), calls=%async_computation.10 | async-start | bytes 1048576 | tf_op jit(solution)/shard_map/all_to_all | solution.py:19
  252.8 18.0 %all-to-all-done.10 = bf16[32,64,128]{2,1,0:T(8,128)(2,1)S(1)} async-done(((bf16[32,64,128]{2,1,0:T(8,128)(2,1)}), bf16[32,64,128]{2,1,0:T(8,128)(2,1)S(1)}, u32[]{:S(2)}, u32[]{:S(2)}) %all-to-all-start.10) | async-done | bytes 524320 | tf_op jit(solution)/shard_map/all_to_all | solution.py:19
  271.7 22.3 %all_to_all.92 = bf16[32,64,128]{2,1,0:T(8,128)(2,1)S(1)} all-to-all(bf16[32,64,128]{2,1,0:T(8,128)(2,1)S(1)} %broadcast_in_dim.102), channel_id=1, replica_groups=mesh['x'=4,'z'=8,'y'=4,'core'=2] {'x','z'}, dimensions={0} | all-to-all | bytes 1048576 | tf_op jit(solution)/shard_map/all_to_all | solution.py:19
  300.5 3.5 collective-permute-done.12
  308.1 22.6 %all_to_all.93 = bf16[32,64,128]{2,1,0:T(8,128)(2,1)S(1)} all-to-all(bf16[32,64,128]{2,1,0:T(8,128)(2,1)S(1)} %bitcast.151), channel_id=1, replica_groups=mesh['x'=4,'z'=8,'y'=4,'core'=2] {'x','z'}, dimensions={0} | all-to-all | bytes 1048576 | tf_op jit(solution)/shard_map/all_to_all | solution.py:19
  330.9 11.3 %all_to_all.94 = bf16[8,64,128]{2,1,0:T(8,128)(2,1)S(1)} all-to-all(bf16[8,64,128]{2,1,0:T(8,128)(2,1)S(1)} %broadcast_in_dim.104), channel_id=1, replica_groups=mesh['x'=4,'z'=8,'y'=4,'core'=2] {'z'}, dimensions={0} | all-to-all | bytes 262144 | tf_op jit(solution)/shard_map/all_to_all | solution.py:19
  355.9 5.0 %all-to-all-start.14 = ((bf16[32,64,128]{2,1,0:T(8,128)(2,1)}), bf16[32,64,128]{2,1,0:T(8,128)(2,1)S(1)}, u32[]{:S(2)}, u32[]{:S(2)}) async-start(bf16[32,64,128]{2,1,0:T(8,128)(2,1)} %multiply_reduce_fusion), calls=%async_computation.14 | async-start | bytes 1048576 | tf_op jit(solution)/shard_map/all_to_all | solution.py:19
  366.7 12.5 %all-to-all-done.14 = bf16[32,64,128]{2,1,0:T(8,128)(2,1)S(1)} async-done(((bf16[32,64,128]{2,1,0:T(8,128)(2,1)}), bf16[32,64,128]{2,1,0:T(8,128)(2,1)S(1)}, u32[]{:S(2)}, u32[]{:S(2)}) %all-to-all-start.14) | async-done | bytes 524320 | tf_op jit(solution)/shard_map/all_to_all | solution.py:19
  385.6 7.2 %all-to-all-done.15 = bf16[4,256,128]{2,1,0:T(8,128)(2,1)S(1)} async-done(((bf16[4,256,128]{2,1,0:T(8,128)(2,1)}), bf16[4,256,128]{2,1,0:T(8,128)(2,1)S(1)}, u32[]{:S(2)}, u32[]{:S(2)}) %all-to-all-start.15) | async-done | bytes 262176 | tf_op jit(solution)/shard_map/all_to_all | solution.py:19
  399.8 6.6 %all-to-all-done.16 = bf16[4,256,128]{2,1,0:T(8,128)(2,1)S(1)} async-done(((bf16[4,256,128]{2,1,0:T(8,128)(2,1)}), bf16[4,256,128]{2,1,0:T(8,128)(2,1)S(1)}, u32[]{:S(2)}, u32[]{:S(2)}) %all-to-all-start.16) | async-done | bytes 262176 | tf_op jit(solution)/shard_map/all_to_all | solution.py:19
  (187 shorter events, 117.0 us)
Async XLA Ops:
  28.9 29.1 %all-to-all-start.2 = ((bf16[32,64,128]{2,1,0:T(8,128)(2,1)}), bf16[32,64,128]{2,1,0:T(8,128)(2,1)S(1)}, u32[]{:S(2)}, u32[]{:S(2)}) async-start(bf16[32,64,128]{2,1,0:T(8,128)(2,1)} %pieces_product.3), calls=%async_computation.2 | async-start | bytes 1048576 | tf_op jit(solution)/shard_map/all_to_all | solution.py:19
  41.0 10.1 %collective-permute-start = (bf16[528,128]{1,0:T(8,128)(2,1)S(1)}, bf16[528,128]{1,0:T(8,128)(2,1)S(1)}, u32[]{:S(2)}, u32[]{:S(2)}) collective-permute-start(bf16[528,128]{1,0:T(8,128)(2,1)S(1)} %get-tuple-element.28), channel_id=1, source_target_pairs={{0,64},{64,128},{128,192},{192,0},{1,65},{65,129},{129,193},{193,1... | collective-permute-start | bytes 405512 | tf_op jit(solution)/shard_map/ppermute | solution.py:51
  42.5 12.4 %collective-permute-start.1 = (bf16[528,128]{1,0:T(8,128)(2,1)S(1)}, bf16[528,128]{1,0:T(8,128)(2,1)S(1)}, u32[]{:S(2)}, u32[]{:S(2)}) collective-permute-start(bf16[528,128]{1,0:T(8,128)(2,1)S(1)} %get-tuple-element.27), channel_id=1, source_target_pairs={{0,128},{64,192},{128,0},{192,64},{1,129},{65,193},{129,1},{193,65... | collective-permute-start | bytes 405512 | tf_op jit(solution)/shard_map/ppermute | solution.py:51
  45.3 9.6 %collective-permute-start.2 = (bf16[528,128]{1,0:T(8,128)(2,1)S(1)}, bf16[528,128]{1,0:T(8,128)(2,1)S(1)}, u32[]{:S(2)}, u32[]{:S(2)}) collective-permute-start(bf16[528,128]{1,0:T(8,128)(2,1)S(1)} %get-tuple-element.26), channel_id=1, source_target_pairs={{0,192},{64,0},{128,64},{192,128},{1,193},{65,1},{129,65},{193,129... | collective-permute-start | bytes 405512 | tf_op jit(solution)/shard_map/ppermute | solution.py:51
  59.4 10.5 %all-to-all-start.3 = ((bf16[4,320,128]{2,1,0:T(8,128)(2,1)}), bf16[4,320,128]{2,1,0:T(8,128)(2,1)S(1)}, u32[]{:S(2)}, u32[]{:S(2)}) async-start(bf16[4,320,128]{2,1,0:T(8,128)(2,1)} %broadcast_in_dim.47), calls=%async_computation.3 | async-start | bytes 655360 | tf_op jit(solution)/shard_map/all_to_all | solution.py:19
  85.5 22.9 %all-to-all-start.5 = ((bf16[32,64,128]{2,1,0:T(8,128)(2,1)}), bf16[32,64,128]{2,1,0:T(8,128)(2,1)S(1)}, u32[]{:S(2)}, u32[]{:S(2)}) async-start(bf16[32,64,128]{2,1,0:T(8,128)(2,1)} %broadcast_in_dim.94), calls=%async_computation.5 | async-start | bytes 1048576 | tf_op jit(solution)/shard_map/all_to_all | solution.py:19
  113.2 6.8 %collective-permute-start.3 = (bf16[256,128]{1,0:T(8,128)(2,1)S(1)}, bf16[256,128]{1,0:T(8,128)(2,1)S(1)}, u32[]{:S(2)}, u32[]{:S(2)}) collective-permute-start(bf16[256,128]{1,0:T(8,128)(2,1)S(1)} %dynamic-slice_reduce_fusion.4), channel_id=1, source_target_pairs={{0,2},{2,4},{4,6},{6,0},{1,3},{3,5},{5,7},{7,1},{8,10},{10,12},{12... | collective-permute-start | bytes 196616 | tf_op jit(solution)/shard_map/ppermute | solution.py:51
  113.9 6.2 %collective-permute-start.4 = (bf16[256,128]{1,0:T(8,128)(2,1)S(1)}, bf16[256,128]{1,0:T(8,128)(2,1)S(1)}, u32[]{:S(2)}, u32[]{:S(2)}) collective-permute-start(bf16[256,128]{1,0:T(8,128)(2,1)S(1)} %dynamic-slice_reduce_fusion.4), channel_id=1, source_target_pairs={{0,4},{2,6},{4,0},{6,2},{1,5},{3,7},{5,1},{7,3},{8,12},{10,14},{12... | collective-permute-start | bytes 196616 | tf_op jit(solution)/shard_map/ppermute | solution.py:51
  174.5 5.9 %collective-permute-start.6 = (bf16[256,128]{1,0:T(8,128)(2,1)S(1)}, bf16[256,128]{1,0:T(8,128)(2,1)S(1)}, u32[]{:S(2)}, u32[]{:S(2)}) collective-permute-start(bf16[256,128]{1,0:T(8,128)(2,1)S(1)} %dynamic-slice_reduce_fusion.3), channel_id=1, source_target_pairs={{0,2},{2,4},{4,6},{6,0},{1,3},{3,5},{5,7},{7,1},{8,10},{10,12},{12... | collective-permute-start | bytes 196616 | tf_op jit(solution)/shard_map/ppermute | solution.py:51
  175.7 6.4 %collective-permute-start.7 = (bf16[256,128]{1,0:T(8,128)(2,1)S(1)}, bf16[256,128]{1,0:T(8,128)(2,1)S(1)}, u32[]{:S(2)}, u32[]{:S(2)}) collective-permute-start(bf16[256,128]{1,0:T(8,128)(2,1)S(1)} %dynamic-slice_reduce_fusion.3), channel_id=1, source_target_pairs={{0,4},{2,6},{4,0},{6,2},{1,5},{3,7},{5,1},{7,3},{8,12},{10,14},{12... | collective-permute-start | bytes 196616 | tf_op jit(solution)/shard_map/ppermute | solution.py:51
  235.3 6.0 %collective-permute-start.10 = (bf16[256,128]{1,0:T(8,128)(2,1)S(1)}, bf16[256,128]{1,0:T(8,128)(2,1)S(1)}, u32[]{:S(2)}, u32[]{:S(2)}) collective-permute-start(bf16[256,128]{1,0:T(8,128)(2,1)S(1)} %dynamic-slice_reduce_fusion.2), channel_id=1, source_target_pairs={{0,4},{2,6},{4,0},{6,2},{1,5},{3,7},{5,1},{7,3},{8,12},{10,14},{12... | collective-permute-start | bytes 196616 | tf_op jit(solution)/shard_map/ppermute | solution.py:51
  238.8 5.5 %collective-permute-start.9 = (bf16[256,128]{1,0:T(8,128)(2,1)S(1)}, bf16[256,128]{1,0:T(8,128)(2,1)S(1)}, u32[]{:S(2)}, u32[]{:S(2)}) collective-permute-start(bf16[256,128]{1,0:T(8,128)(2,1)S(1)} %dynamic-slice_reduce_fusion.2), channel_id=1, source_target_pairs={{0,2},{2,4},{4,6},{6,0},{1,3},{3,5},{5,7},{7,1},{8,10},{10,12},{12... | collective-permute-start | bytes 196616 | tf_op jit(solution)/shard_map/ppermute | solution.py:51
  247.8 22.9 %all-to-all-start.10 = ((bf16[32,64,128]{2,1,0:T(8,128)(2,1)}), bf16[32,64,128]{2,1,0:T(8,128)(2,1)S(1)}, u32[]{:S(2)}, u32[]{:S(2)}) async-start(bf16[32,64,128]{2,1,0:T(8,128)(2,1)} %bitcast.37), calls=%async_computation.10 | async-start | bytes 1048576 | tf_op jit(solution)/shard_map/all_to_all | solution.py:19
  297.2 6.8 %collective-permute-start.12 = (bf16[256,128]{1,0:T(8,128)(2,1)S(1)}, bf16[256,128]{1,0:T(8,128)(2,1)S(1)}, u32[]{:S(2)}, u32[]{:S(2)}) collective-permute-start(bf16[256,128]{1,0:T(8,128)(2,1)S(1)} %dynamic-slice_reduce_fusion.1), channel_id=1, source_target_pairs={{0,2},{2,4},{4,6},{6,0},{1,3},{3,5},{5,7},{7,1},{8,10},{10,12},{12... | collective-permute-start | bytes 196616 | tf_op jit(solution)/shard_map/ppermute | solution.py:51
  297.3 6.8 %collective-permute-start.13 = (bf16[256,128]{1,0:T(8,128)(2,1)S(1)}, bf16[256,128]{1,0:T(8,128)(2,1)S(1)}, u32[]{:S(2)}, u32[]{:S(2)}) collective-permute-start(bf16[256,128]{1,0:T(8,128)(2,1)S(1)} %dynamic-slice_reduce_fusion.1), channel_id=1, source_target_pairs={{0,4},{2,6},{4,0},{6,2},{1,5},{3,7},{5,1},{7,3},{8,12},{10,14},{12... | collective-permute-start | bytes 196616 | tf_op jit(solution)/shard_map/ppermute | solution.py:51
  299.1 5.6 %collective-permute-start.14 = (bf16[256,128]{1,0:T(8,128)(2,1)S(1)}, bf16[256,128]{1,0:T(8,128)(2,1)S(1)}, u32[]{:S(2)}, u32[]{:S(2)}) collective-permute-start(bf16[256,128]{1,0:T(8,128)(2,1)S(1)} %dynamic-slice_reduce_fusion.1), channel_id=1, source_target_pairs={{0,6},{2,0},{4,2},{6,4},{1,7},{3,1},{5,3},{7,5},{8,14},{10,8},{12,... | collective-permute-start | bytes 196616 | tf_op jit(solution)/shard_map/ppermute | solution.py:51
  344.5 5.9 %collective-permute-start.15 = (bf16[256,128]{1,0:T(8,128)(2,1)S(1)}, bf16[256,128]{1,0:T(8,128)(2,1)S(1)}, u32[]{:S(2)}, u32[]{:S(2)}) collective-permute-start(bf16[256,128]{1,0:T(8,128)(2,1)S(1)} %dynamic-slice_reduce_fusion), channel_id=1, source_target_pairs={{0,2},{2,4},{4,6},{6,0},{1,3},{3,5},{5,7},{7,1},{8,10},{10,12},{12... | collective-permute-start | bytes 196616 | tf_op jit(solution)/shard_map/ppermute | solution.py:51
  345.6 6.3 %collective-permute-start.16 = (bf16[256,128]{1,0:T(8,128)(2,1)S(1)}, bf16[256,128]{1,0:T(8,128)(2,1)S(1)}, u32[]{:S(2)}, u32[]{:S(2)}) collective-permute-start(bf16[256,128]{1,0:T(8,128)(2,1)S(1)} %dynamic-slice_reduce_fusion), channel_id=1, source_target_pairs={{0,4},{2,6},{4,0},{6,2},{1,5},{3,7},{5,1},{7,3},{8,12},{10,14},{12... | collective-permute-start | bytes 196616 | tf_op jit(solution)/shard_map/ppermute | solution.py:51
  355.9 23.3 %all-to-all-start.14 = ((bf16[32,64,128]{2,1,0:T(8,128)(2,1)}), bf16[32,64,128]{2,1,0:T(8,128)(2,1)S(1)}, u32[]{:S(2)}, u32[]{:S(2)}) async-start(bf16[32,64,128]{2,1,0:T(8,128)(2,1)} %multiply_reduce_fusion), calls=%async_computation.14 | async-start | bytes 1048576 | tf_op jit(solution)/shard_map/all_to_all | solution.py:19
  362.1 17.7 %collective-permute-start.20 = (bf16[16,128]{1,0:T(8,128)(2,1)S(1)}, bf16[16,128]{1,0:T(8,128)(2,1)S(1)}, u32[]{:S(2)}, u32[]{:S(2)}) collective-permute-start(bf16[16,128]{1,0:T(8,128)(2,1)S(1)} %get-tuple-element.35), channel_id=1, source_target_pairs={{0,192},{64,0},{128,64},{192,128},{1,193},{65,1},{129,65},{193,129... | collective-permute-start | bytes 12296 | tf_op jit(solution)/shard_map/ppermute | solution.py:51
  365.1 14.8 %collective-permute-start.21 = (bf16[16,128]{1,0:T(8,128)(2,1)S(1)}, bf16[16,128]{1,0:T(8,128)(2,1)S(1)}, u32[]{:S(2)}, u32[]{:S(2)}) collective-permute-start(bf16[16,128]{1,0:T(8,128)(2,1)S(1)} %get-tuple-element.34), channel_id=1, source_target_pairs={{0,128},{64,192},{128,0},{192,64},{1,129},{65,193},{129,1},{193,65... | collective-permute-start | bytes 12296 | tf_op jit(solution)/shard_map/ppermute | solution.py:51
  365.8 19.8 %collective-permute-start.22 = (bf16[16,128]{1,0:T(8,128)(2,1)S(1)}, bf16[16,128]{1,0:T(8,128)(2,1)S(1)}, u32[]{:S(2)}, u32[]{:S(2)}) collective-permute-start(bf16[16,128]{1,0:T(8,128)(2,1)S(1)} %get-tuple-element.32), channel_id=1, source_target_pairs={{0,64},{64,128},{128,192},{192,0},{1,65},{65,129},{129,193},{193,1... | collective-permute-start | bytes 12296 | tf_op jit(solution)/shard_map/ppermute | solution.py:51
  382.1 10.6 %all-to-all-start.15 = ((bf16[4,256,128]{2,1,0:T(8,128)(2,1)}), bf16[4,256,128]{2,1,0:T(8,128)(2,1)S(1)}, u32[]{:S(2)}, u32[]{:S(2)}) async-start(bf16[4,256,128]{2,1,0:T(8,128)(2,1)} %fusion.1), calls=%async_computation.15 | async-start | bytes 524288 | tf_op jit(solution)/shard_map/all_to_all | solution.py:19
  395.7 10.6 %all-to-all-start.16 = ((bf16[4,256,128]{2,1,0:T(8,128)(2,1)}), bf16[4,256,128]{2,1,0:T(8,128)(2,1)S(1)}, u32[]{:S(2)}, u32[]{:S(2)}) async-start(bf16[4,256,128]{2,1,0:T(8,128)(2,1)} %fusion), calls=%async_computation.16 | async-start | bytes 524288 | tf_op jit(solution)/shard_map/all_to_all | solution.py:19
  (25 other events, 424.6 us)

commit v2 on v1

--- a/solution.py
+++ b/solution.py
@@ -114,58 +114,55 @@
     group = count // groups
     slots = rows // BLOCK
 
-    parts = 2
-    part = rows // parts
-
     def kernel(position_ref, matrix_ref, columns_ref, *refs):
-        out_ref, held_ref, sems, sum_ref = refs[-4:]
-        moves = {}
-        for member in range(count):
-            for piece in range(parts):
-                at = pl.ds(piece * part, part)
-                moves[member, piece] = pltpu.make_async_copy(
-                    matrix_ref.at[member, at], held_ref.at[member, at], sems.at[member * parts + piece]
-                )
-                moves[member, piece].start()
-        for unit in range(groups):
-            for piece in range(parts):
-                at = slice(piece * part, piece * part + part)
-                result = refs[0][unit, at].astype(F32) if carried is not None else jnp.zeros((part, probes), F32)
-                for member in range(unit * group, unit * group + group):
-                    moves[member, piece].wait()
-                    result += product(held_ref[member, at], columns_ref[member])
-                if carried is not None:
-                    out_ref[unit, at] = result.astype(dtype)
-                else:
-                    sum_ref[unit, at] = result
-            if carried is None:
+        out_ref, sum_ref = refs[-2:]
+        member = pl.program_id(0) % group
+
+        @pl.when(member == 0)
+        def _():
+            if carried is not None:
+                sum_ref[...] = refs[0][0].astype(F32)
+            else:
                 landed_ref, own_ref = refs[:2]
                 here, core, row = position_ref[0], position_ref[1], position_ref[2]
+                sum_ref[...] = jnp.zeros_like(sum_ref)
                 for slot in range(slots):
                     at = pl.ds(pl.multiple_of(slot * BLOCK + core * HALF, HALF), HALF)
-                    sum_ref[unit, at, :] += jnp.where(here > 0, landed_ref[unit * slots + slot].astype(F32), 0.0)
+                    sum_ref[at, :] += jnp.where(here > 0, landed_ref[slot].astype(F32), 0.0)
                 own = rows // ROWS
                 at = pl.ds(pl.multiple_of(row * own, own), own)
-                sum_ref[unit, at, :] -= own_ref[unit].astype(F32)
-                out_ref[unit] = sum_ref[unit].astype(dtype)
-
-    vmem = pl.BlockSpec(memory_space=pltpu.VMEM)
-    operands = (landed, own_probes) if carried is None else (carried,)
-    scratch = [
-        pltpu.VMEM((count, rows, depth), BF16),
-        pltpu.SemaphoreType.DMA((count * parts,)),
-        pltpu.VMEM((groups, rows, probes), F32),
+                sum_ref[at, :] -= own_ref[0].astype(F32)
+
+        sum_ref[...] += product(matrix_ref[0], columns_ref[0])
+
+        @pl.when(member == group - 1)
+        def _():
+            out_ref[0] = sum_ref[...].astype(dtype)
+
+    in_specs = [
+        pl.BlockSpec(memory_space=pltpu.SMEM),
+        pl.BlockSpec((1, rows, depth), lambda s: (s, 0, 0)),
+        pl.BlockSpec((1, depth, probes), lambda s: (s, 0, 0)),
     ]
+    if carried is None:
+        in_specs += [
+            pl.BlockSpec((slots, HALF, probes), lambda s: (s // group, 0, 0)),
+            pl.BlockSpec((1, rows // ROWS, probes), lambda s: (s // group, 0, 0)),
+        ]
+        operands = (landed, own_probes)
+    else:
+        in_specs += [pl.BlockSpec((1, rows, probes), lambda s: (s // group, 0, 0))]
+        operands = (carried,)
     return pl.pallas_call(
         kernel,
         out_shape=jax.ShapeDtypeStruct((groups, rows, probes), dtype),
-        in_specs=[pl.BlockSpec(memory_space=pltpu.SMEM), pl.BlockSpec(memory_space=pltpu.HBM), vmem]
-        + [vmem] * len(operands),
-        out_specs=vmem,
-        scratch_shapes=scratch,
+        grid=(count,),
+        in_specs=in_specs,
+        out_specs=pl.BlockSpec((1, rows, probes), lambda s: (s // group, 0, 0)),
+        scratch_shapes=[pltpu.VMEM((rows, probes), F32)],
         compiler_params=LIMITS,
         name="forward_total",
-    )(position, pltpu.with_memory_space_constraint(matrix, pltpu.HBM), columns, *operands)
+    )(position, matrix, columns, *operands)
 
 
 def backward(matrix, rows_in, depth_at_once=512):
@@ -294,8 +291,9 @@
     chosen = (slot[None, :] == jnp.arange(4, dtype=jnp.int32)[:, None]).astype(F32)
 
     held = row_gather(leaf_probes[0])
-    leaf_solved = pieces_product(inverse, held, 1)[0]
-    updates = pieces_product(panel, row_gather(leaf_solved), LEAVES)
+    solved_copies = pieces_product(inverse, held, 4)
+    leaf_solved = solved_copies[0]
+    updates = pieces_product(panel, both_cores(swap(solved_copies, "y")), LEAVES)
     updates, tiles, pieces = lax.optimization_barrier((updates, lower_inverse, lower_probes))
     lower_held = jnp.concatenate([tiles, pieces], axis=1)
     leaving = [take(lower_held, (x + step) % 4, 0) for step in range(4)]
@@ -323,7 +321,7 @@
 
     def early_root(pair):
         block, _ = lax.optimization_barrier((lower_block, pair))
-        return forward_total(lower_to_root, block, at_level(3), landed, root_probes[None], None, F32)
+        return forward_total(lower_to_root, block, at_level(3), landed, root_probes[None], None, BF16)
 
     to_middle = forward_total(lower_to_middle, lower_block, at_level(2), landed, middle_probes, None, BF16).reshape(512, probes)
     middle_half, to_root = row_half_sum(to_middle, core, early_root)

time: 409 us -> 407 us (level)
  no operation moved by 1% of the time
where the time goes in v2:
time: 407 us; the launch traced here: 406 us
  blocking collectives  205 us (50%)
  waiting for transfers between devices  101 us (25%)
  starting transfers between devices  66.3 us (16%)
  Pallas kernels  15.3 us (4%)
  local copies, waits for them, and re-layouts  8.32 us (2%)
  other arithmetic  7.64 us (2%)
    all_to_all x10, blocking collectives, swap(): return lax.all_to_all(pieces, axes, split_axis=0, concat_axis=0, tiled=True)  179 us
    all_to_all x7, waiting for transfers between devices, swap(): return lax.all_to_all(pieces, axes, split_axis=0, concat_axis=0, tiled=True)  70.9 us
    all_to_all x7, starting transfers between devices, swap(): return lax.all_to_all(pieces, axes, split_axis=0, concat_axis=0, tiled=True)  37.3 us
    ppermute x21, starting transfers between devices, shift(): return lax.ppermute(piece, axis, [(i, (i + step) % 4) for i in range(4)])  28.8 us
    ppermute x21, waiting for transfers between devices, shift(): return lax.ppermute(piece, axis, [(i, (i + step) % 4) for i in range(4)])  27.6 us
    all_gather x13, blocking collectives, both_cores(): return lax.all_gather(piece, 'core', axis=0, tiled=False)  26.3 us
  transfers between devices with their start and end apart: 30, of which 24 were waited for; matrix products, arithmetic and copies ran while one was open for 1% of the time, Pallas kernels for 1%

profile of v2, /device:TPU:32, one launch (start us, length us, event | category | flops | bytes accessed | tf_op | source)
XLA Modules:
  0.0 405.5 jit_solution(8291552334425299908)
XLA Ops:
  1.6 10.9 %all_to_all.85 = bf16[4,256,128]{2,1,0:T(8,128)(2,1)S(1)} all-to-all(bf16[4,256,128]{2,1,0:T(8,128)(2,1)S(1)} %broadcast_in_dim.39), channel_id=1, replica_groups=mesh['x'=4,'z'=8,'y'=4,'core'=2] {'y'}, dimensions={0} | all-to-all | bytes 524288 | tf_op jit(solution)/shard_map/all_to_all | solution.py:19
  15.3 9.8 %all_to_all.86 = bf16[4,256,128]{2,1,0:T(8,128)(2,1)S(1)} all-to-all(bf16[4,256,128]{2,1,0:T(8,128)(2,1)S(1)} %pieces_product.2), channel_id=1, replica_groups=mesh['x'=4,'z'=8,'y'=4,'core'=2] {'y'}, dimensions={0} | all-to-all | bytes 524288 | tf_op jit(solution)/shard_map/all_to_all | solution.py:19
  28.4 11.2 %all-to-all-start.2 = ((bf16[32,64,128]{2,1,0:T(8,128)(2,1)}), bf16[32,64,128]{2,1,0:T(8,128)(2,1)S(1)}, u32[]{:S(2)}, u32[]{:S(2)}) async-start(bf16[32,64,128]{2,1,0:T(8,128)(2,1)} %pieces_product.3), calls=%async_computation.2 | async-start | bytes 1048576 | tf_op jit(solution)/shard_map/all_to_all | solution.py:19
  46.2 4.4 %collective-permute-done = bf16[528,128]{1,0:T(8,128)(2,1)S(1)} collective-permute-done((bf16[528,128]{1,0:T(8,128)(2,1)S(1)}, bf16[528,128]{1,0:T(8,128)(2,1)S(1)}, u32[]{:S(2)}, u32[]{:S(2)}) %collective-permute-start) | collective-permute-done | bytes 135200 | tf_op jit(solution)/shard_map/ppermute | solution.py:51
  50.6 3.8 collective-permute-done.1
  58.9 3.5 all-to-all-start.3
  62.5 6.9 %all-to-all-done.3 = bf16[4,320,128]{2,1,0:T(8,128)(2,1)S(1)} async-done(((bf16[4,320,128]{2,1,0:T(8,128)(2,1)}), bf16[4,320,128]{2,1,0:T(8,128)(2,1)S(1)}, u32[]{:S(2)}, u32[]{:S(2)}) %all-to-all-start.3) | async-done | bytes 327712 | tf_op jit(solution)/shard_map/all_to_all | solution.py:19
  71.9 12.3 %all_to_all.87 = bf16[8,64,128]{2,1,0:T(8,128)(2,1)S(1)} all-to-all(bf16[8,64,128]{2,1,0:T(8,128)(2,1)S(1)} %bitcast.164), channel_id=1, replica_groups=mesh['x'=4,'z'=8,'y'=4,'core'=2] {'z'}, dimensions={0} | all-to-all | bytes 262144 | tf_op jit(solution)/shard_map/all_to_all | solution.py:19
  85.1 5.8 %all-to-all-start.5 = ((bf16[32,64,128]{2,1,0:T(8,128)(2,1)}), bf16[32,64,128]{2,1,0:T(8,128)(2,1)S(1)}, u32[]{:S(2)}, u32[]{:S(2)}) async-start(bf16[32,64,128]{2,1,0:T(8,128)(2,1)} %broadcast_in_dim.42), calls=%async_computation.5 | async-start | bytes 1048576 | tf_op jit(solution)/shard_map/all_to_all | solution.py:19
  91.0 16.9 %all-to-all-done.5 = bf16[32,64,128]{2,1,0:T(8,128)(2,1)S(1)} async-done(((bf16[32,64,128]{2,1,0:T(8,128)(2,1)}), bf16[32,64,128]{2,1,0:T(8,128)(2,1)S(1)}, u32[]{:S(2)}, u32[]{:S(2)}) %all-to-all-start.5) | async-done | bytes 524320 | tf_op jit(solution)/shard_map/all_to_all | solution.py:19
  123.2 22.7 %all_to_all.88 = bf16[32,64,128]{2,1,0:T(8,128)(2,1)S(1)} all-to-all(bf16[32,64,128]{2,1,0:T(8,128)(2,1)S(1)} %bitcast.152), channel_id=1, replica_groups=mesh['x'=4,'z'=8,'y'=4,'core'=2] {'x','z'}, dimensions={0} | all-to-all | bytes 1048576 | tf_op jit(solution)/shard_map/all_to_all | solution.py:19
  146.2 22.1 %all_to_all.89 = bf16[32,64,128]{2,1,0:T(8,128)(2,1)S(1)} all-to-all(bf16[32,64,128]{2,1,0:T(8,128)(2,1)S(1)} %broadcast_in_dim.44), channel_id=1, replica_groups=mesh['x'=4,'z'=8,'y'=4,'core'=2] {'x','z'}, dimensions={0} | all-to-all | bytes 1048576 | tf_op jit(solution)/shard_map/all_to_all | solution.py:19
  185.1 22.7 %all_to_all.90 = bf16[32,64,128]{2,1,0:T(8,128)(2,1)} all-to-all(bf16[32,64,128]{2,1,0:T(8,128)(2,1)S(1)} %bitcast.154), channel_id=1, replica_groups=mesh['x'=4,'z'=8,'y'=4,'core'=2] {'x','z'}, dimensions={0} | all-to-all | bytes 1048576 | tf_op jit(solution)/shard_map/all_to_all | solution.py:19
  209.1 22.1 %all_to_all.91 = bf16[32,64,128]{2,1,0:T(8,128)(2,1)S(1)} all-to-all(bf16[32,64,128]{2,1,0:T(8,128)(2,1)S(1)} %broadcast_in_dim.89), channel_id=1, replica_groups=mesh['x'=4,'z'=8,'y'=4,'core'=2] {'x','z'}, dimensions={0} | all-to-all | bytes 1048576 | tf_op jit(solution)/shard_map/all_to_all | solution.py:19
  246.2 5.0 %all-to-all-start.10 = ((bf16[32,64,128]{2,1,0:T(8,128)(2,1)}), bf16[32,64,128]{2,1,0:T(8,128)(2,1)S(1)}, u32[]{:S(2)}, u32[]{:S(2)}) async-start(bf16[32,64,128]{2,1,0:T(8,128)(2,1)} %bitcast.36), calls=%async_computation.10 | async-start | bytes 1048576 | tf_op jit(solution)/shard_map/all_to_all | solution.py:19
  251.2 18.0 %all-to-all-done.10 = bf16[32,64,128]{2,1,0:T(8,128)(2,1)S(1)} async-done(((bf16[32,64,128]{2,1,0:T(8,128)(2,1)}), bf16[32,64,128]{2,1,0:T(8,128)(2,1)S(1)}, u32[]{:S(2)}, u32[]{:S(2)}) %all-to-all-start.10) | async-done | bytes 524320 | tf_op jit(solution)/shard_map/all_to_all | solution.py:19
  270.1 22.3 %all_to_all.92 = bf16[32,64,128]{2,1,0:T(8,128)(2,1)S(1)} all-to-all(bf16[32,64,128]{2,1,0:T(8,128)(2,1)S(1)} %broadcast_in_dim.93), channel_id=1, replica_groups=mesh['x'=4,'z'=8,'y'=4,'core'=2] {'x','z'}, dimensions={0} | all-to-all | bytes 1048576 | tf_op jit(solution)/shard_map/all_to_all | solution.py:19
  299.0 3.5 collective-permute-done.12
  306.5 22.6 %all_to_all.93 = bf16[32,64,128]{2,1,0:T(8,128)(2,1)S(1)} all-to-all(bf16[32,64,128]{2,1,0:T(8,128)(2,1)S(1)} %bitcast.150), channel_id=1, replica_groups=mesh['x'=4,'z'=8,'y'=4,'core'=2] {'x','z'}, dimensions={0} | all-to-all | bytes 1048576 | tf_op jit(solution)/shard_map/all_to_all | solution.py:19
  329.3 11.3 %all_to_all.94 = bf16[8,64,128]{2,1,0:T(8,128)(2,1)S(1)} all-to-all(bf16[8,64,128]{2,1,0:T(8,128)(2,1)S(1)} %broadcast_in_dim.95), channel_id=1, replica_groups=mesh['x'=4,'z'=8,'y'=4,'core'=2] {'z'}, dimensions={0} | all-to-all | bytes 262144 | tf_op jit(solution)/shard_map/all_to_all | solution.py:19
  354.4 5.0 %all-to-all-start.14 = ((bf16[32,64,128]{2,1,0:T(8,128)(2,1)}), bf16[32,64,128]{2,1,0:T(8,128)(2,1)S(1)}, u32[]{:S(2)}, u32[]{:S(2)}) async-start(bf16[32,64,128]{2,1,0:T(8,128)(2,1)} %multiply_reduce_fusion), calls=%async_computation.14 | async-start | bytes 1048576 | tf_op jit(solution)/shard_map/all_to_all | solution.py:19
  365.5 12.3 %all-to-all-done.14 = bf16[32,64,128]{2,1,0:T(8,128)(2,1)S(1)} async-done(((bf16[32,64,128]{2,1,0:T(8,128)(2,1)}), bf16[32,64,128]{2,1,0:T(8,128)(2,1)S(1)}, u32[]{:S(2)}, u32[]{:S(2)}) %all-to-all-start.14) | async-done | bytes 524320 | tf_op jit(solution)/shard_map/all_to_all | solution.py:19
  384.1 7.2 %all-to-all-done.15 = bf16[4,256,128]{2,1,0:T(8,128)(2,1)S(1)} async-done(((bf16[4,256,128]{2,1,0:T(8,128)(2,1)}), bf16[4,256,128]{2,1,0:T(8,128)(2,1)S(1)}, u32[]{:S(2)}, u32[]{:S(2)}) %all-to-all-start.15) | async-done | bytes 262176 | tf_op jit(solution)/shard_map/all_to_all | solution.py:19
  398.3 6.6 %all-to-all-done.16 = bf16[4,256,128]{2,1,0:T(8,128)(2,1)S(1)} async-done(((bf16[4,256,128]{2,1,0:T(8,128)(2,1)}), bf16[4,256,128]{2,1,0:T(8,128)(2,1)S(1)}, u32[]{:S(2)}, u32[]{:S(2)}) %all-to-all-start.16) | async-done | bytes 262176 | tf_op jit(solution)/shard_map/all_to_all | solution.py:19
  (190 shorter events, 115.5 us)
Async XLA Ops:
  28.4 29.1 %all-to-all-start.2 = ((bf16[32,64,128]{2,1,0:T(8,128)(2,1)}), bf16[32,64,128]{2,1,0:T(8,128)(2,1)S(1)}, u32[]{:S(2)}, u32[]{:S(2)}) async-start(bf16[32,64,128]{2,1,0:T(8,128)(2,1)} %pieces_product.3), calls=%async_computation.2 | async-start | bytes 1048576 | tf_op jit(solution)/shard_map/all_to_all | solution.py:19
  40.5 10.1 %collective-permute-start = (bf16[528,128]{1,0:T(8,128)(2,1)S(1)}, bf16[528,128]{1,0:T(8,128)(2,1)S(1)}, u32[]{:S(2)}, u32[]{:S(2)}) collective-permute-start(bf16[528,128]{1,0:T(8,128)(2,1)S(1)} %get-tuple-element.28), channel_id=1, source_target_pairs={{0,64},{64,128},{128,192},{192,0},{1,65},{65,129},{129,193},{193,1... | collective-permute-start | bytes 405512 | tf_op jit(solution)/shard_map/ppermute | solution.py:51
  42.1 12.4 %collective-permute-start.1 = (bf16[528,128]{1,0:T(8,128)(2,1)S(1)}, bf16[528,128]{1,0:T(8,128)(2,1)S(1)}, u32[]{:S(2)}, u32[]{:S(2)}) collective-permute-start(bf16[528,128]{1,0:T(8,128)(2,1)S(1)} %get-tuple-element.27), channel_id=1, source_target_pairs={{0,128},{64,192},{128,0},{192,64},{1,129},{65,193},{129,1},{193,65... | collective-permute-start | bytes 405512 | tf_op jit(solution)/shard_map/ppermute | solution.py:51
  44.8 9.6 %collective-permute-start.2 = (bf16[528,128]{1,0:T(8,128)(2,1)S(1)}, bf16[528,128]{1,0:T(8,128)(2,1)S(1)}, u32[]{:S(2)}, u32[]{:S(2)}) collective-permute-start(bf16[528,128]{1,0:T(8,128)(2,1)S(1)} %get-tuple-element.26), channel_id=1, source_target_pairs={{0,192},{64,0},{128,64},{192,128},{1,193},{65,1},{129,65},{193,129... | collective-permute-start | bytes 405512 | tf_op jit(solution)/shard_map/ppermute | solution.py:51
  58.9 10.5 %all-to-all-start.3 = ((bf16[4,320,128]{2,1,0:T(8,128)(2,1)}), bf16[4,320,128]{2,1,0:T(8,128)(2,1)S(1)}, u32[]{:S(2)}, u32[]{:S(2)}) async-start(bf16[4,320,128]{2,1,0:T(8,128)(2,1)} %broadcast_in_dim.41), calls=%async_computation.3 | async-start | bytes 655360 | tf_op jit(solution)/shard_map/all_to_all | solution.py:19
  85.1 22.9 %all-to-all-start.5 = ((bf16[32,64,128]{2,1,0:T(8,128)(2,1)}), bf16[32,64,128]{2,1,0:T(8,128)(2,1)S(1)}, u32[]{:S(2)}, u32[]{:S(2)}) async-start(bf16[32,64,128]{2,1,0:T(8,128)(2,1)} %broadcast_in_dim.42), calls=%async_computation.5 | async-start | bytes 1048576 | tf_op jit(solution)/shard_map/all_to_all | solution.py:19
  112.9 6.8 %collective-permute-start.3 = (bf16[256,128]{1,0:T(8,128)(2,1)S(1)}, bf16[256,128]{1,0:T(8,128)(2,1)S(1)}, u32[]{:S(2)}, u32[]{:S(2)}) collective-permute-start(bf16[256,128]{1,0:T(8,128)(2,1)S(1)} %dynamic-slice_reduce_fusion.4), channel_id=1, source_target_pairs={{0,2},{2,4},{4,6},{6,0},{1,3},{3,5},{5,7},{7,1},{8,10},{10,12},{12... | collective-permute-start | bytes 196616 | tf_op jit(solution)/shard_map/ppermute | solution.py:51
  113.6 6.2 %collective-permute-start.4 = (bf16[256,128]{1,0:T(8,128)(2,1)S(1)}, bf16[256,128]{1,0:T(8,128)(2,1)S(1)}, u32[]{:S(2)}, u32[]{:S(2)}) collective-permute-start(bf16[256,128]{1,0:T(8,128)(2,1)S(1)} %dynamic-slice_reduce_fusion.4), channel_id=1, source_target_pairs={{0,4},{2,6},{4,0},{6,2},{1,5},{3,7},{5,1},{7,3},{8,12},{10,14},{12... | collective-permute-start | bytes 196616 | tf_op jit(solution)/shard_map/ppermute | solution.py:51
  173.6 5.6 %collective-permute-start.6 = (bf16[256,128]{1,0:T(8,128)(2,1)S(1)}, bf16[256,128]{1,0:T(8,128)(2,1)S(1)}, u32[]{:S(2)}, u32[]{:S(2)}) collective-permute-start(bf16[256,128]{1,0:T(8,128)(2,1)S(1)} %dynamic-slice_reduce_fusion.3), channel_id=1, source_target_pairs={{0,2},{2,4},{4,6},{6,0},{1,3},{3,5},{5,7},{7,1},{8,10},{10,12},{12... | collective-permute-start | bytes 196616 | tf_op jit(solution)/shard_map/ppermute | solution.py:51
  174.7 6.5 %collective-permute-start.7 = (bf16[256,128]{1,0:T(8,128)(2,1)S(1)}, bf16[256,128]{1,0:T(8,128)(2,1)S(1)}, u32[]{:S(2)}, u32[]{:S(2)}) collective-permute-start(bf16[256,128]{1,0:T(8,128)(2,1)S(1)} %dynamic-slice_reduce_fusion.3), channel_id=1, source_target_pairs={{0,4},{2,6},{4,0},{6,2},{1,5},{3,7},{5,1},{7,3},{8,12},{10,14},{12... | collective-permute-start | bytes 196616 | tf_op jit(solution)/shard_map/ppermute | solution.py:51
  234.3 6.0 %collective-permute-start.10 = (bf16[256,128]{1,0:T(8,128)(2,1)S(1)}, bf16[256,128]{1,0:T(8,128)(2,1)S(1)}, u32[]{:S(2)}, u32[]{:S(2)}) collective-permute-start(bf16[256,128]{1,0:T(8,128)(2,1)S(1)} %dynamic-slice_reduce_fusion.2), channel_id=1, source_target_pairs={{0,4},{2,6},{4,0},{6,2},{1,5},{3,7},{5,1},{7,3},{8,12},{10,14},{12... | collective-permute-start | bytes 196616 | tf_op jit(solution)/shard_map/ppermute | solution.py:51
  237.2 5.5 %collective-permute-start.9 = (bf16[256,128]{1,0:T(8,128)(2,1)S(1)}, bf16[256,128]{1,0:T(8,128)(2,1)S(1)}, u32[]{:S(2)}, u32[]{:S(2)}) collective-permute-start(bf16[256,128]{1,0:T(8,128)(2,1)S(1)} %dynamic-slice_reduce_fusion.2), channel_id=1, source_target_pairs={{0,2},{2,4},{4,6},{6,0},{1,3},{3,5},{5,7},{7,1},{8,10},{10,12},{12... | collective-permute-start | bytes 196616 | tf_op jit(solution)/shard_map/ppermute | solution.py:51
  246.2 22.9 %all-to-all-start.10 = ((bf16[32,64,128]{2,1,0:T(8,128)(2,1)}), bf16[32,64,128]{2,1,0:T(8,128)(2,1)S(1)}, u32[]{:S(2)}, u32[]{:S(2)}) async-start(bf16[32,64,128]{2,1,0:T(8,128)(2,1)} %bitcast.36), calls=%async_computation.10 | async-start | bytes 1048576 | tf_op jit(solution)/shard_map/all_to_all | solution.py:19
  295.6 6.8 %collective-permute-start.12 = (bf16[256,128]{1,0:T(8,128)(2,1)S(1)}, bf16[256,128]{1,0:T(8,128)(2,1)S(1)}, u32[]{:S(2)}, u32[]{:S(2)}) collective-permute-start(bf16[256,128]{1,0:T(8,128)(2,1)S(1)} %dynamic-slice_reduce_fusion.1), channel_id=1, source_target_pairs={{0,2},{2,4},{4,6},{6,0},{1,3},{3,5},{5,7},{7,1},{8,10},{10,12},{12... | collective-permute-start | bytes 196616 | tf_op jit(solution)/shard_map/ppermute | solution.py:51
  295.7 6.8 %collective-permute-start.13 = (bf16[256,128]{1,0:T(8,128)(2,1)S(1)}, bf16[256,128]{1,0:T(8,128)(2,1)S(1)}, u32[]{:S(2)}, u32[]{:S(2)}) collective-permute-start(bf16[256,128]{1,0:T(8,128)(2,1)S(1)} %dynamic-slice_reduce_fusion.1), channel_id=1, source_target_pairs={{0,4},{2,6},{4,0},{6,2},{1,5},{3,7},{5,1},{7,3},{8,12},{10,14},{12... | collective-permute-start | bytes 196616 | tf_op jit(solution)/shard_map/ppermute | solution.py:51
  297.7 5.3 %collective-permute-start.14 = (bf16[256,128]{1,0:T(8,128)(2,1)S(1)}, bf16[256,128]{1,0:T(8,128)(2,1)S(1)}, u32[]{:S(2)}, u32[]{:S(2)}) collective-permute-start(bf16[256,128]{1,0:T(8,128)(2,1)S(1)} %dynamic-slice_reduce_fusion.1), channel_id=1, source_target_pairs={{0,6},{2,0},{4,2},{6,4},{1,7},{3,1},{5,3},{7,5},{8,14},{10,8},{12,... | collective-permute-start | bytes 196616 | tf_op jit(solution)/shard_map/ppermute | solution.py:51
  343.0 5.8 %collective-permute-start.15 = (bf16[256,128]{1,0:T(8,128)(2,1)S(1)}, bf16[256,128]{1,0:T(8,128)(2,1)S(1)}, u32[]{:S(2)}, u32[]{:S(2)}) collective-permute-start(bf16[256,128]{1,0:T(8,128)(2,1)S(1)} %dynamic-slice_reduce_fusion), channel_id=1, source_target_pairs={{0,2},{2,4},{4,6},{6,0},{1,3},{3,5},{5,7},{7,1},{8,10},{10,12},{12... | collective-permute-start | bytes 196616 | tf_op jit(solution)/shard_map/ppermute | solution.py:51
  344.1 6.3 %collective-permute-start.16 = (bf16[256,128]{1,0:T(8,128)(2,1)S(1)}, bf16[256,128]{1,0:T(8,128)(2,1)S(1)}, u32[]{:S(2)}, u32[]{:S(2)}) collective-permute-start(bf16[256,128]{1,0:T(8,128)(2,1)S(1)} %dynamic-slice_reduce_fusion), channel_id=1, source_target_pairs={{0,4},{2,6},{4,0},{6,2},{1,5},{3,7},{5,1},{7,3},{8,12},{10,14},{12... | collective-permute-start | bytes 196616 | tf_op jit(solution)/shard_map/ppermute | solution.py:51
  354.4 23.3 %all-to-all-start.14 = ((bf16[32,64,128]{2,1,0:T(8,128)(2,1)}), bf16[32,64,128]{2,1,0:T(8,128)(2,1)S(1)}, u32[]{:S(2)}, u32[]{:S(2)}) async-start(bf16[32,64,128]{2,1,0:T(8,128)(2,1)} %multiply_reduce_fusion), calls=%async_computation.14 | async-start | bytes 1048576 | tf_op jit(solution)/shard_map/all_to_all | solution.py:19
  360.7 17.7 %collective-permute-start.20 = (bf16[16,128]{1,0:T(8,128)(2,1)S(1)}, bf16[16,128]{1,0:T(8,128)(2,1)S(1)}, u32[]{:S(2)}, u32[]{:S(2)}) collective-permute-start(bf16[16,128]{1,0:T(8,128)(2,1)S(1)} %get-tuple-element.35), channel_id=1, source_target_pairs={{0,192},{64,0},{128,64},{192,128},{1,193},{65,1},{129,65},{193,129... | collective-permute-start | bytes 12296 | tf_op jit(solution)/shard_map/ppermute | solution.py:51
  363.8 14.6 %collective-permute-start.21 = (bf16[16,128]{1,0:T(8,128)(2,1)S(1)}, bf16[16,128]{1,0:T(8,128)(2,1)S(1)}, u32[]{:S(2)}, u32[]{:S(2)}) collective-permute-start(bf16[16,128]{1,0:T(8,128)(2,1)S(1)} %get-tuple-element.34), channel_id=1, source_target_pairs={{0,128},{64,192},{128,0},{192,64},{1,129},{65,193},{129,1},{193,65... | collective-permute-start | bytes 12296 | tf_op jit(solution)/shard_map/ppermute | solution.py:51
  364.6 19.5 %collective-permute-start.22 = (bf16[16,128]{1,0:T(8,128)(2,1)S(1)}, bf16[16,128]{1,0:T(8,128)(2,1)S(1)}, u32[]{:S(2)}, u32[]{:S(2)}) collective-permute-start(bf16[16,128]{1,0:T(8,128)(2,1)S(1)} %get-tuple-element.32), channel_id=1, source_target_pairs={{0,64},{64,128},{128,192},{192,0},{1,65},{65,129},{129,193},{193,1... | collective-permute-start | bytes 12296 | tf_op jit(solution)/shard_map/ppermute | solution.py:51
  380.7 10.6 %all-to-all-start.15 = ((bf16[4,256,128]{2,1,0:T(8,128)(2,1)}), bf16[4,256,128]{2,1,0:T(8,128)(2,1)S(1)}, u32[]{:S(2)}, u32[]{:S(2)}) async-start(bf16[4,256,128]{2,1,0:T(8,128)(2,1)} %fusion.1), calls=%async_computation.15 | async-start | bytes 524288 | tf_op jit(solution)/shard_map/all_to_all | solution.py:19
  394.2 10.6 %all-to-all-start.16 = ((bf16[4,256,128]{2,1,0:T(8,128)(2,1)}), bf16[4,256,128]{2,1,0:T(8,128)(2,1)S(1)}, u32[]{:S(2)}, u32[]{:S(2)}) async-start(bf16[4,256,128]{2,1,0:T(8,128)(2,1)} %fusion), calls=%async_computation.16 | async-start | bytes 524288 | tf_op jit(solution)/shard_map/all_to_all | solution.py:19
  (27 other events, 505.5 us)

commit v3 on v1

--- a/solution.py
+++ b/solution.py
@@ -114,46 +114,42 @@
     group = count // groups
     slots = rows // BLOCK
 
-    parts = 2
-    part = rows // parts
-
     def kernel(position_ref, matrix_ref, columns_ref, *refs):
         out_ref, held_ref, sems, sum_ref = refs[-4:]
-        moves = {}
+
+        def move(member):
+            return pltpu.make_async_copy(matrix_ref.at[member], held_ref.at[member], sems.at[member])
+
         for member in range(count):
-            for piece in range(parts):
-                at = pl.ds(piece * part, part)
-                moves[member, piece] = pltpu.make_async_copy(
-                    matrix_ref.at[member, at], held_ref.at[member, at], sems.at[member * parts + piece]
-                )
-                moves[member, piece].start()
-        for unit in range(groups):
-            for piece in range(parts):
-                at = slice(piece * part, piece * part + part)
-                result = refs[0][unit, at].astype(F32) if carried is not None else jnp.zeros((part, probes), F32)
-                for member in range(unit * group, unit * group + group):
-                    moves[member, piece].wait()
-                    result += product(held_ref[member, at], columns_ref[member])
-                if carried is not None:
-                    out_ref[unit, at] = result.astype(dtype)
-                else:
-                    sum_ref[unit, at] = result
-            if carried is None:
-                landed_ref, own_ref = refs[:2]
-                here, core, row = position_ref[0], position_ref[1], position_ref[2]
+            move(member).start()
+        if carried is not None:
+            sum_ref[...] = refs[0][...].astype(F32)
+        else:
+            landed_ref, own_ref = refs[:2]
+            here, core, row = position_ref[0], position_ref[1], position_ref[2]
+            own = rows // ROWS
+            sum_ref[...] = jnp.zeros_like(sum_ref)
+            for unit in range(groups):
                 for slot in range(slots):
                     at = pl.ds(pl.multiple_of(slot * BLOCK + core * HALF, HALF), HALF)
                     sum_ref[unit, at, :] += jnp.where(here > 0, landed_ref[unit * slots + slot].astype(F32), 0.0)
-                own = rows // ROWS
                 at = pl.ds(pl.multiple_of(row * own, own), own)
                 sum_ref[unit, at, :] -= own_ref[unit].astype(F32)
-                out_ref[unit] = sum_ref[unit].astype(dtype)
+
+        def step(member, carry):
+            move(member).wait()
+            unit = lax.div(member, group)
+            sum_ref[unit] += product(held_ref[member], columns_ref[member])
+            return carry
+
+        lax.fori_loop(0, count, step, 0)
+        out_ref[...] = sum_ref[...].astype(dtype)
 
     vmem = pl.BlockSpec(memory_space=pltpu.VMEM)
     operands = (landed, own_probes) if carried is None else (carried,)
     scratch = [
         pltpu.VMEM((count, rows, depth), BF16),
-        pltpu.SemaphoreType.DMA((count * parts,)),
+        pltpu.SemaphoreType.DMA((count,)),
         pltpu.VMEM((groups, rows, probes), F32),
     ]
     return pl.pallas_call(
@@ -294,8 +290,9 @@
     chosen = (slot[None, :] == jnp.arange(4, dtype=jnp.int32)[:, None]).astype(F32)
 
     held = row_gather(leaf_probes[0])
-    leaf_solved = pieces_product(inverse, held, 1)[0]
-    updates = pieces_product(panel, row_gather(leaf_solved), LEAVES)
+    solved_copies = pieces_product(inverse, held, 4)
+    leaf_solved = solved_copies[0]
+    updates = pieces_product(panel, both_cores(swap(solved_copies, "y")), LEAVES)
     updates, tiles, pieces = lax.optimization_barrier((updates, lower_inverse, lower_probes))
     lower_held = jnp.concatenate([tiles, pieces], axis=1)
     leaving = [take(lower_held, (x + step) % 4, 0) for step in range(4)]
@@ -323,7 +320,7 @@
 
     def early_root(pair):
         block, _ = lax.optimization_barrier((lower_block, pair))
-        return forward_total(lower_to_root, block, at_level(3), landed, root_probes[None], None, F32)
+        return forward_total(lower_to_root, block, at_level(3), landed, root_probes[None], None, BF16)
 
     to_middle = forward_total(lower_to_middle, lower_block, at_level(2), landed, middle_probes, None, BF16).reshape(512, probes)
     middle_half, to_root = row_half_sum(to_middle, core, early_root)

time: 409 us -> 406 us (level)
  no operation moved by 1% of the time
where the time goes in v3:
time: 406 us; the launch traced here: 405 us
  blocking collectives  205 us (50%)
  waiting for transfers between devices  100 us (25%)
  starting transfers between devices  66.7 us (16%)
  Pallas kernels  18.6 us (5%)
  other arithmetic  7.65 us (2%)
  local copies, waits for them, and re-layouts  5.25 us (1%)
    all_to_all x10, blocking collectives, swap(): return lax.all_to_all(pieces, axes, split_axis=0, concat_axis=0, tiled=True)  179 us
    all_to_all x7, waiting for transfers between devices, swap(): return lax.all_to_all(pieces, axes, split_axis=0, concat_axis=0, tiled=True)  70.9 us
    all_to_all x7, starting transfers between devices, swap(): return lax.all_to_all(pieces, axes, split_axis=0, concat_axis=0, tiled=True)  37.3 us
    ppermute x21, starting transfers between devices, shift(): return lax.ppermute(piece, axis, [(i, (i + step) % 4) for i in range(4)])  29.3 us
    ppermute x21, waiting for transfers between devices, shift(): return lax.ppermute(piece, axis, [(i, (i + step) % 4) for i in range(4)])  26.4 us
    all_gather x13, blocking collectives, both_cores(): return lax.all_gather(piece, 'core', axis=0, tiled=False)  26.3 us
    pallas_call x3, Pallas kernels, forward_total(): pl.pallas_call(kernel, out_shape=jax.ShapeDtypeStruct((groups, rows, prob...  8.18 us
  transfers between devices with their start and end apart: 30, of which 24 were waited for; matrix products, arithmetic and copies ran while one was open for 1% of the time, Pallas kernels for 1%

profile of v3, /device:TPU:32, one launch (start us, length us, event | category | flops | bytes accessed | tf_op | source)
XLA Modules:
  0.0 405.0 jit_solution(3907050669654413584)
XLA Ops:
  1.6 10.9 %all_to_all.85 = bf16[4,256,128]{2,1,0:T(8,128)(2,1)S(1)} all-to-all(bf16[4,256,128]{2,1,0:T(8,128)(2,1)S(1)} %broadcast_in_dim.39), channel_id=1, replica_groups=mesh['x'=4,'z'=8,'y'=4,'core'=2] {'y'}, dimensions={0} | all-to-all | bytes 524288 | tf_op jit(solution)/shard_map/all_to_all | solution.py:19
  15.3 9.8 %all_to_all.86 = bf16[4,256,128]{2,1,0:T(8,128)(2,1)S(1)} all-to-all(bf16[4,256,128]{2,1,0:T(8,128)(2,1)S(1)} %pieces_product.2), channel_id=1, replica_groups=mesh['x'=4,'z'=8,'y'=4,'core'=2] {'y'}, dimensions={0} | all-to-all | bytes 524288 | tf_op jit(solution)/shard_map/all_to_all | solution.py:19
  28.4 11.2 %all-to-all-start.2 = ((bf16[32,64,128]{2,1,0:T(8,128)(2,1)}), bf16[32,64,128]{2,1,0:T(8,128)(2,1)S(1)}, u32[]{:S(2)}, u32[]{:S(2)}) async-start(bf16[32,64,128]{2,1,0:T(8,128)(2,1)} %pieces_product.3), calls=%async_computation.2 | async-start | bytes 1048576 | tf_op jit(solution)/shard_map/all_to_all | solution.py:19
  46.2 4.4 %collective-permute-done = bf16[528,128]{1,0:T(8,128)(2,1)S(1)} collective-permute-done((bf16[528,128]{1,0:T(8,128)(2,1)S(1)}, bf16[528,128]{1,0:T(8,128)(2,1)S(1)}, u32[]{:S(2)}, u32[]{:S(2)}) %collective-permute-start) | collective-permute-done | bytes 135200 | tf_op jit(solution)/shard_map/ppermute | solution.py:51
  50.6 3.8 collective-permute-done.1
  58.9 3.5 all-to-all-start.3
  62.5 6.9 %all-to-all-done.3 = bf16[4,320,128]{2,1,0:T(8,128)(2,1)S(1)} async-done(((bf16[4,320,128]{2,1,0:T(8,128)(2,1)}), bf16[4,320,128]{2,1,0:T(8,128)(2,1)S(1)}, u32[]{:S(2)}, u32[]{:S(2)}) %all-to-all-start.3) | async-done | bytes 327712 | tf_op jit(solution)/shard_map/all_to_all | solution.py:19
  71.8 12.3 %all_to_all.87 = bf16[8,64,128]{2,1,0:T(8,128)(2,1)S(1)} all-to-all(bf16[8,64,128]{2,1,0:T(8,128)(2,1)S(1)} %bitcast.164), channel_id=1, replica_groups=mesh['x'=4,'z'=8,'y'=4,'core'=2] {'z'}, dimensions={0} | all-to-all | bytes 262144 | tf_op jit(solution)/shard_map/all_to_all | solution.py:19
  85.1 5.8 %all-to-all-start.5 = ((bf16[32,64,128]{2,1,0:T(8,128)(2,1)}), bf16[32,64,128]{2,1,0:T(8,128)(2,1)S(1)}, u32[]{:S(2)}, u32[]{:S(2)}) async-start(bf16[32,64,128]{2,1,0:T(8,128)(2,1)} %broadcast_in_dim.42), calls=%async_computation.5 | async-start | bytes 1048576 | tf_op jit(solution)/shard_map/all_to_all | solution.py:19
  91.0 16.9 %all-to-all-done.5 = bf16[32,64,128]{2,1,0:T(8,128)(2,1)S(1)} async-done(((bf16[32,64,128]{2,1,0:T(8,128)(2,1)}), bf16[32,64,128]{2,1,0:T(8,128)(2,1)S(1)}, u32[]{:S(2)}, u32[]{:S(2)}) %all-to-all-start.5) | async-done | bytes 524320 | tf_op jit(solution)/shard_map/all_to_all | solution.py:19
  122.9 22.7 %all_to_all.88 = bf16[32,64,128]{2,1,0:T(8,128)(2,1)S(1)} all-to-all(bf16[32,64,128]{2,1,0:T(8,128)(2,1)S(1)} %bitcast.152), channel_id=1, replica_groups=mesh['x'=4,'z'=8,'y'=4,'core'=2] {'x','z'}, dimensions={0} | all-to-all | bytes 1048576 | tf_op jit(solution)/shard_map/all_to_all | solution.py:19
  145.8 22.1 %all_to_all.89 = bf16[32,64,128]{2,1,0:T(8,128)(2,1)S(1)} all-to-all(bf16[32,64,128]{2,1,0:T(8,128)(2,1)S(1)} %broadcast_in_dim.44), channel_id=1, replica_groups=mesh['x'=4,'z'=8,'y'=4,'core'=2] {'x','z'}, dimensions={0} | all-to-all | bytes 1048576 | tf_op jit(solution)/shard_map/all_to_all | solution.py:19
  184.3 22.7 %all_to_all.90 = bf16[32,64,128]{2,1,0:T(8,128)(2,1)} all-to-all(bf16[32,64,128]{2,1,0:T(8,128)(2,1)S(1)} %bitcast.154), channel_id=1, replica_groups=mesh['x'=4,'z'=8,'y'=4,'core'=2] {'x','z'}, dimensions={0} | all-to-all | bytes 1048576 | tf_op jit(solution)/shard_map/all_to_all | solution.py:19
  208.3 22.1 %all_to_all.91 = bf16[32,64,128]{2,1,0:T(8,128)(2,1)S(1)} all-to-all(bf16[32,64,128]{2,1,0:T(8,128)(2,1)S(1)} %broadcast_in_dim.89), channel_id=1, replica_groups=mesh['x'=4,'z'=8,'y'=4,'core'=2] {'x','z'}, dimensions={0} | all-to-all | bytes 1048576 | tf_op jit(solution)/shard_map/all_to_all | solution.py:19
  245.6 5.0 %all-to-all-start.10 = ((bf16[32,64,128]{2,1,0:T(8,128)(2,1)}), bf16[32,64,128]{2,1,0:T(8,128)(2,1)S(1)}, u32[]{:S(2)}, u32[]{:S(2)}) async-start(bf16[32,64,128]{2,1,0:T(8,128)(2,1)} %bitcast.36), calls=%async_computation.10 | async-start | bytes 1048576 | tf_op jit(solution)/shard_map/all_to_all | solution.py:19
  250.6 18.0 %all-to-all-done.10 = bf16[32,64,128]{2,1,0:T(8,128)(2,1)S(1)} async-done(((bf16[32,64,128]{2,1,0:T(8,128)(2,1)}), bf16[32,64,128]{2,1,0:T(8,128)(2,1)S(1)}, u32[]{:S(2)}, u32[]{:S(2)}) %all-to-all-start.10) | async-done | bytes 524320 | tf_op jit(solution)/shard_map/all_to_all | solution.py:19
  269.5 22.3 %all_to_all.92 = bf16[32,64,128]{2,1,0:T(8,128)(2,1)S(1)} all-to-all(bf16[32,64,128]{2,1,0:T(8,128)(2,1)S(1)} %broadcast_in_dim.93), channel_id=1, replica_groups=mesh['x'=4,'z'=8,'y'=4,'core'=2] {'x','z'}, dimensions={0} | all-to-all | bytes 1048576 | tf_op jit(solution)/shard_map/all_to_all | solution.py:19
  298.4 3.5 collective-permute-done.12
  306.0 22.6 %all_to_all.93 = bf16[32,64,128]{2,1,0:T(8,128)(2,1)S(1)} all-to-all(bf16[32,64,128]{2,1,0:T(8,128)(2,1)S(1)} %bitcast.150), channel_id=1, replica_groups=mesh['x'=4,'z'=8,'y'=4,'core'=2] {'x','z'}, dimensions={0} | all-to-all | bytes 1048576 | tf_op jit(solution)/shard_map/all_to_all | solution.py:19
  328.7 11.3 %all_to_all.94 = bf16[8,64,128]{2,1,0:T(8,128)(2,1)S(1)} all-to-all(bf16[8,64,128]{2,1,0:T(8,128)(2,1)S(1)} %broadcast_in_dim.95), channel_id=1, replica_groups=mesh['x'=4,'z'=8,'y'=4,'core'=2] {'z'}, dimensions={0} | all-to-all | bytes 262144 | tf_op jit(solution)/shard_map/all_to_all | solution.py:19
  353.8 5.0 %all-to-all-start.14 = ((bf16[32,64,128]{2,1,0:T(8,128)(2,1)}), bf16[32,64,128]{2,1,0:T(8,128)(2,1)S(1)}, u32[]{:S(2)}, u32[]{:S(2)}) async-start(bf16[32,64,128]{2,1,0:T(8,128)(2,1)} %multiply_reduce_fusion), calls=%async_computation.14 | async-start | bytes 1048576 | tf_op jit(solution)/shard_map/all_to_all | solution.py:19
  364.9 12.3 %all-to-all-done.14 = bf16[32,64,128]{2,1,0:T(8,128)(2,1)S(1)} async-done(((bf16[32,64,128]{2,1,0:T(8,128)(2,1)}), bf16[32,64,128]{2,1,0:T(8,128)(2,1)S(1)}, u32[]{:S(2)}, u32[]{:S(2)}) %all-to-all-start.14) | async-done | bytes 524320 | tf_op jit(solution)/shard_map/all_to_all | solution.py:19
  383.6 7.2 %all-to-all-done.15 = bf16[4,256,128]{2,1,0:T(8,128)(2,1)S(1)} async-done(((bf16[4,256,128]{2,1,0:T(8,128)(2,1)}), bf16[4,256,128]{2,1,0:T(8,128)(2,1)S(1)}, u32[]{:S(2)}, u32[]{:S(2)}) %all-to-all-start.15) | async-done | bytes 262176 | tf_op jit(solution)/shard_map/all_to_all | solution.py:19
  397.7 6.6 %all-to-all-done.16 = bf16[4,256,128]{2,1,0:T(8,128)(2,1)S(1)} async-done(((bf16[4,256,128]{2,1,0:T(8,128)(2,1)}), bf16[4,256,128]{2,1,0:T(8,128)(2,1)S(1)}, u32[]{:S(2)}, u32[]{:S(2)}) %all-to-all-start.16) | async-done | bytes 262176 | tf_op jit(solution)/shard_map/all_to_all | solution.py:19
  (184 shorter events, 114.9 us)
Async XLA Ops:
  28.4 29.1 %all-to-all-start.2 = ((bf16[32,64,128]{2,1,0:T(8,128)(2,1)}), bf16[32,64,128]{2,1,0:T(8,128)(2,1)S(1)}, u32[]{:S(2)}, u32[]{:S(2)}) async-start(bf16[32,64,128]{2,1,0:T(8,128)(2,1)} %pieces_product.3), calls=%async_computation.2 | async-start | bytes 1048576 | tf_op jit(solution)/shard_map/all_to_all | solution.py:19
  40.5 10.1 %collective-permute-start = (bf16[528,128]{1,0:T(8,128)(2,1)S(1)}, bf16[528,128]{1,0:T(8,128)(2,1)S(1)}, u32[]{:S(2)}, u32[]{:S(2)}) collective-permute-start(bf16[528,128]{1,0:T(8,128)(2,1)S(1)} %get-tuple-element.28), channel_id=1, source_target_pairs={{0,64},{64,128},{128,192},{192,0},{1,65},{65,129},{129,193},{193,1... | collective-permute-start | bytes 405512 | tf_op jit(solution)/shard_map/ppermute | solution.py:51
  42.1 12.4 %collective-permute-start.1 = (bf16[528,128]{1,0:T(8,128)(2,1)S(1)}, bf16[528,128]{1,0:T(8,128)(2,1)S(1)}, u32[]{:S(2)}, u32[]{:S(2)}) collective-permute-start(bf16[528,128]{1,0:T(8,128)(2,1)S(1)} %get-tuple-element.27), channel_id=1, source_target_pairs={{0,128},{64,192},{128,0},{192,64},{1,129},{65,193},{129,1},{193,65... | collective-permute-start | bytes 405512 | tf_op jit(solution)/shard_map/ppermute | solution.py:51
  44.8 9.6 %collective-permute-start.2 = (bf16[528,128]{1,0:T(8,128)(2,1)S(1)}, bf16[528,128]{1,0:T(8,128)(2,1)S(1)}, u32[]{:S(2)}, u32[]{:S(2)}) collective-permute-start(bf16[528,128]{1,0:T(8,128)(2,1)S(1)} %get-tuple-element.26), channel_id=1, source_target_pairs={{0,192},{64,0},{128,64},{192,128},{1,193},{65,1},{129,65},{193,129... | collective-permute-start | bytes 405512 | tf_op jit(solution)/shard_map/ppermute | solution.py:51
  58.9 10.5 %all-to-all-start.3 = ((bf16[4,320,128]{2,1,0:T(8,128)(2,1)}), bf16[4,320,128]{2,1,0:T(8,128)(2,1)S(1)}, u32[]{:S(2)}, u32[]{:S(2)}) async-start(bf16[4,320,128]{2,1,0:T(8,128)(2,1)} %broadcast_in_dim.41), calls=%async_computation.3 | async-start | bytes 655360 | tf_op jit(solution)/shard_map/all_to_all | solution.py:19
  85.1 22.9 %all-to-all-start.5 = ((bf16[32,64,128]{2,1,0:T(8,128)(2,1)}), bf16[32,64,128]{2,1,0:T(8,128)(2,1)S(1)}, u32[]{:S(2)}, u32[]{:S(2)}) async-start(bf16[32,64,128]{2,1,0:T(8,128)(2,1)} %broadcast_in_dim.42), calls=%async_computation.5 | async-start | bytes 1048576 | tf_op jit(solution)/shard_map/all_to_all | solution.py:19
  112.5 6.8 %collective-permute-start.3 = (bf16[256,128]{1,0:T(8,128)(2,1)S(1)}, bf16[256,128]{1,0:T(8,128)(2,1)S(1)}, u32[]{:S(2)}, u32[]{:S(2)}) collective-permute-start(bf16[256,128]{1,0:T(8,128)(2,1)S(1)} %dynamic-slice_reduce_fusion.4), channel_id=1, source_target_pairs={{0,2},{2,4},{4,6},{6,0},{1,3},{3,5},{5,7},{7,1},{8,10},{10,12},{12... | collective-permute-start | bytes 196616 | tf_op jit(solution)/shard_map/ppermute | solution.py:51
  113.2 6.2 %collective-permute-start.4 = (bf16[256,128]{1,0:T(8,128)(2,1)S(1)}, bf16[256,128]{1,0:T(8,128)(2,1)S(1)}, u32[]{:S(2)}, u32[]{:S(2)}) collective-permute-start(bf16[256,128]{1,0:T(8,128)(2,1)S(1)} %dynamic-slice_reduce_fusion.4), channel_id=1, source_target_pairs={{0,4},{2,6},{4,0},{6,2},{1,5},{3,7},{5,1},{7,3},{8,12},{10,14},{12... | collective-permute-start | bytes 196616 | tf_op jit(solution)/shard_map/ppermute | solution.py:51
  172.9 5.8 %collective-permute-start.6 = (bf16[256,128]{1,0:T(8,128)(2,1)S(1)}, bf16[256,128]{1,0:T(8,128)(2,1)S(1)}, u32[]{:S(2)}, u32[]{:S(2)}) collective-permute-start(bf16[256,128]{1,0:T(8,128)(2,1)S(1)} %dynamic-slice_reduce_fusion.3), channel_id=1, source_target_pairs={{0,2},{2,4},{4,6},{6,0},{1,3},{3,5},{5,7},{7,1},{8,10},{10,12},{12... | collective-permute-start | bytes 196616 | tf_op jit(solution)/shard_map/ppermute | solution.py:51
  174.0 6.4 %collective-permute-start.7 = (bf16[256,128]{1,0:T(8,128)(2,1)S(1)}, bf16[256,128]{1,0:T(8,128)(2,1)S(1)}, u32[]{:S(2)}, u32[]{:S(2)}) collective-permute-start(bf16[256,128]{1,0:T(8,128)(2,1)S(1)} %dynamic-slice_reduce_fusion.3), channel_id=1, source_target_pairs={{0,4},{2,6},{4,0},{6,2},{1,5},{3,7},{5,1},{7,3},{8,12},{10,14},{12... | collective-permute-start | bytes 196616 | tf_op jit(solution)/shard_map/ppermute | solution.py:51
  233.5 6.0 %collective-permute-start.10 = (bf16[256,128]{1,0:T(8,128)(2,1)S(1)}, bf16[256,128]{1,0:T(8,128)(2,1)S(1)}, u32[]{:S(2)}, u32[]{:S(2)}) collective-permute-start(bf16[256,128]{1,0:T(8,128)(2,1)S(1)} %dynamic-slice_reduce_fusion.2), channel_id=1, source_target_pairs={{0,4},{2,6},{4,0},{6,2},{1,5},{3,7},{5,1},{7,3},{8,12},{10,14},{12... | collective-permute-start | bytes 196616 | tf_op jit(solution)/shard_map/ppermute | solution.py:51
  236.6 5.5 %collective-permute-start.9 = (bf16[256,128]{1,0:T(8,128)(2,1)S(1)}, bf16[256,128]{1,0:T(8,128)(2,1)S(1)}, u32[]{:S(2)}, u32[]{:S(2)}) collective-permute-start(bf16[256,128]{1,0:T(8,128)(2,1)S(1)} %dynamic-slice_reduce_fusion.2), channel_id=1, source_target_pairs={{0,2},{2,4},{4,6},{6,0},{1,3},{3,5},{5,7},{7,1},{8,10},{10,12},{12... | collective-permute-start | bytes 196616 | tf_op jit(solution)/shard_map/ppermute | solution.py:51
  245.6 22.9 %all-to-all-start.10 = ((bf16[32,64,128]{2,1,0:T(8,128)(2,1)}), bf16[32,64,128]{2,1,0:T(8,128)(2,1)S(1)}, u32[]{:S(2)}, u32[]{:S(2)}) async-start(bf16[32,64,128]{2,1,0:T(8,128)(2,1)} %bitcast.36), calls=%async_computation.10 | async-start | bytes 1048576 | tf_op jit(solution)/shard_map/all_to_all | solution.py:19
  295.1 6.8 %collective-permute-start.12 = (bf16[256,128]{1,0:T(8,128)(2,1)S(1)}, bf16[256,128]{1,0:T(8,128)(2,1)S(1)}, u32[]{:S(2)}, u32[]{:S(2)}) collective-permute-start(bf16[256,128]{1,0:T(8,128)(2,1)S(1)} %dynamic-slice_reduce_fusion.1), channel_id=1, source_target_pairs={{0,2},{2,4},{4,6},{6,0},{1,3},{3,5},{5,7},{7,1},{8,10},{10,12},{12... | collective-permute-start | bytes 196616 | tf_op jit(solution)/shard_map/ppermute | solution.py:51
  295.1 6.8 %collective-permute-start.13 = (bf16[256,128]{1,0:T(8,128)(2,1)S(1)}, bf16[256,128]{1,0:T(8,128)(2,1)S(1)}, u32[]{:S(2)}, u32[]{:S(2)}) collective-permute-start(bf16[256,128]{1,0:T(8,128)(2,1)S(1)} %dynamic-slice_reduce_fusion.1), channel_id=1, source_target_pairs={{0,4},{2,6},{4,0},{6,2},{1,5},{3,7},{5,1},{7,3},{8,12},{10,14},{12... | collective-permute-start | bytes 196616 | tf_op jit(solution)/shard_map/ppermute | solution.py:51
  297.0 5.5 %collective-permute-start.14 = (bf16[256,128]{1,0:T(8,128)(2,1)S(1)}, bf16[256,128]{1,0:T(8,128)(2,1)S(1)}, u32[]{:S(2)}, u32[]{:S(2)}) collective-permute-start(bf16[256,128]{1,0:T(8,128)(2,1)S(1)} %dynamic-slice_reduce_fusion.1), channel_id=1, source_target_pairs={{0,6},{2,0},{4,2},{6,4},{1,7},{3,1},{5,3},{7,5},{8,14},{10,8},{12,... | collective-permute-start | bytes 196616 | tf_op jit(solution)/shard_map/ppermute | solution.py:51
  342.5 5.9 %collective-permute-start.15 = (bf16[256,128]{1,0:T(8,128)(2,1)S(1)}, bf16[256,128]{1,0:T(8,128)(2,1)S(1)}, u32[]{:S(2)}, u32[]{:S(2)}) collective-permute-start(bf16[256,128]{1,0:T(8,128)(2,1)S(1)} %dynamic-slice_reduce_fusion), channel_id=1, source_target_pairs={{0,2},{2,4},{4,6},{6,0},{1,3},{3,5},{5,7},{7,1},{8,10},{10,12},{12... | collective-permute-start | bytes 196616 | tf_op jit(solution)/shard_map/ppermute | solution.py:51
  343.6 6.3 %collective-permute-start.16 = (bf16[256,128]{1,0:T(8,128)(2,1)S(1)}, bf16[256,128]{1,0:T(8,128)(2,1)S(1)}, u32[]{:S(2)}, u32[]{:S(2)}) collective-permute-start(bf16[256,128]{1,0:T(8,128)(2,1)S(1)} %dynamic-slice_reduce_fusion), channel_id=1, source_target_pairs={{0,4},{2,6},{4,0},{6,2},{1,5},{3,7},{5,1},{7,3},{8,12},{10,14},{12... | collective-permute-start | bytes 196616 | tf_op jit(solution)/shard_map/ppermute | solution.py:51
  353.8 23.3 %all-to-all-start.14 = ((bf16[32,64,128]{2,1,0:T(8,128)(2,1)}), bf16[32,64,128]{2,1,0:T(8,128)(2,1)S(1)}, u32[]{:S(2)}, u32[]{:S(2)}) async-start(bf16[32,64,128]{2,1,0:T(8,128)(2,1)} %multiply_reduce_fusion), calls=%async_computation.14 | async-start | bytes 1048576 | tf_op jit(solution)/shard_map/all_to_all | solution.py:19
  360.1 17.7 %collective-permute-start.20 = (bf16[16,128]{1,0:T(8,128)(2,1)S(1)}, bf16[16,128]{1,0:T(8,128)(2,1)S(1)}, u32[]{:S(2)}, u32[]{:S(2)}) collective-permute-start(bf16[16,128]{1,0:T(8,128)(2,1)S(1)} %get-tuple-element.35), channel_id=1, source_target_pairs={{0,192},{64,0},{128,64},{192,128},{1,193},{65,1},{129,65},{193,129... | collective-permute-start | bytes 12296 | tf_op jit(solution)/shard_map/ppermute | solution.py:51
  363.2 14.6 %collective-permute-start.21 = (bf16[16,128]{1,0:T(8,128)(2,1)S(1)}, bf16[16,128]{1,0:T(8,128)(2,1)S(1)}, u32[]{:S(2)}, u32[]{:S(2)}) collective-permute-start(bf16[16,128]{1,0:T(8,128)(2,1)S(1)} %get-tuple-element.34), channel_id=1, source_target_pairs={{0,128},{64,192},{128,0},{192,64},{1,129},{65,193},{129,1},{193,65... | collective-permute-start | bytes 12296 | tf_op jit(solution)/shard_map/ppermute | solution.py:51
  364.0 19.5 %collective-permute-start.22 = (bf16[16,128]{1,0:T(8,128)(2,1)S(1)}, bf16[16,128]{1,0:T(8,128)(2,1)S(1)}, u32[]{:S(2)}, u32[]{:S(2)}) collective-permute-start(bf16[16,128]{1,0:T(8,128)(2,1)S(1)} %get-tuple-element.32), channel_id=1, source_target_pairs={{0,64},{64,128},{128,192},{192,0},{1,65},{65,129},{129,193},{193,1... | collective-permute-start | bytes 12296 | tf_op jit(solution)/shard_map/ppermute | solution.py:51
  380.1 10.6 %all-to-all-start.15 = ((bf16[4,256,128]{2,1,0:T(8,128)(2,1)}), bf16[4,256,128]{2,1,0:T(8,128)(2,1)S(1)}, u32[]{:S(2)}, u32[]{:S(2)}) async-start(bf16[4,256,128]{2,1,0:T(8,128)(2,1)} %fusion.1), calls=%async_computation.15 | async-start | bytes 524288 | tf_op jit(solution)/shard_map/all_to_all | solution.py:19
  393.7 10.6 %all-to-all-start.16 = ((bf16[4,256,128]{2,1,0:T(8,128)(2,1)}), bf16[4,256,128]{2,1,0:T(8,128)(2,1)S(1)}, u32[]{:S(2)}, u32[]{:S(2)}) async-start(bf16[4,256,128]{2,1,0:T(8,128)(2,1)} %fusion), calls=%async_computation.16 | async-start | bytes 524288 | tf_op jit(solution)/shard_map/all_to_all | solution.py:19
  (24 other events, 469.5 us)
